TPU v7x, 32 devices: a whole 2x2x4 slice. The times are simulated.
32 devices in a mesh: img: 8 (over z, y), ch: 4 (over x, core).
Axes of the slice: x: 2, y: 2, z: 4, core: 2. Of those that a mesh axis runs over, the one named last changes fastest.
Arguments:
- kspace_data: float32 [4, 12, 2, 320, 320], P('ch', None, None, None, 'img'), may hold values from -6 to 6
- coil_maps: float32 [4, 12, 2, 320, 320], P('ch', None, None, 'img'), may hold values from -2.3 to 2.3
- sample_mask: int32 [4, 320, 320], P('ch', None, 'img'), may hold values 0 or 1
- valid_mask: int32 [4, 320, 320], P(None, 'img'), may hold values from 0 to 1, as said below
- target: float32 [4, 2, 320, 320], P('ch', None, 'img'), may hold values from -11.3 to 11.3
- first_weight: float32 [9, 64, 2], P(None, 'ch'), may hold values from -1.5 to 1.5
- middle_weights: float32 [3, 9, 64, 64], P(None, None, 'ch'), may hold values from -0.25 to 0.25
- last_weight: float32 [9, 2, 64], P(None, None, 'ch'), may hold values from -0.25 to 0.25
- norm_params: float32 [4, 2, 64], P(None, None, 'ch'), may hold values from 0.2 to 1.5
- penalty: float32 [1], replicated, may hold values from 0.03 to 0.08
- first_mean: float32 [9, 64, 2], P(None, 'ch'), may hold values from -0.0017089844 to 0.0017089844
- first_square: float32 [9, 64, 2], P(None, 'ch'), may hold values from 1e-08 to 4e-08
- middle_mean: float32 [3, 9, 64, 64], P(None, None, 'ch'), may hold values from -0.0017089844 to 0.0017089844
- middle_square: float32 [3, 9, 64, 64], P(None, None, 'ch'), may hold values from 1e-08 to 4e-08
- last_mean: float32 [9, 2, 64], P(None, None, 'ch'), may hold values from -0.0017089844 to 0.0017089844
- last_square: float32 [9, 2, 64], P(None, None, 'ch'), may hold values from 1e-08 to 4e-08
- norm_mean: float32 [4, 2, 64], P(None, None, 'ch'), may hold values from -0.0017089844 to 0.0017089844
- norm_square: float32 [4, 2, 64], P(None, None, 'ch'), may hold values from 1e-08 to 4e-08
- penalty_mean: float32 [1], replicated, may hold values from -0.3125 to 0.3125
- penalty_square: float32 [1], replicated, may hold values from 0.00025 to 0.001
- step_count: int32 [1], replicated, may hold values from 1 to 20
Outputs:
- loss_value: float32 [], replicated
- first_new: float32 [9, 64, 2], P(None, 'ch')
- first_mean_new: float32 [9, 64, 2], P(None, 'ch')
- first_square_new: float32 [9, 64, 2], P(None, 'ch')
- middle_new: float32 [3, 9, 64, 64], P(None, None, 'ch')
- middle_mean_new: float32 [3, 9, 64, 64], P(None, None, 'ch')
- middle_square_new: float32 [3, 9, 64, 64], P(None, None, 'ch')
- last_new: float32 [9, 2, 64], P(None, None, 'ch')
- last_mean_new: float32 [9, 2, 64], P(None, None, 'ch')
- last_square_new: float32 [9, 2, 64], P(None, None, 'ch')
- norm_new: float32 [4, 2, 64], P(None, None, 'ch')
- norm_mean_new: float32 [4, 2, 64], P(None, None, 'ch')
- norm_square_new: float32 [4, 2, 64], P(None, None, 'ch')
- penalty_state: float32 [3], replicated
Inputs may be any that keep to these rules, and one draw needn't show every extreme that they name: `valid_mask`: each image's ones fill one rectangle of at least 160 rows and 160 columns.
All inputs are finite; a program needn't handle non-finite values. No bound on the sum of `sample_mask` on one device may be relied on, other than what follows from the above.
Results may differ from a plain program's by a relative error of at most 0.0053.
Values may be sent and summed in bfloat16 or wider, within the bound.
No kernel may reach another device: no remote copies, remote signals or barrier semaphores. Data moves between devices by JAX's collectives and lax.ppermute only.
A program may use at most 576 MiB of HBM per device.

v0:
```python
import math

import jax
import jax.numpy as jnp
from jax import lax
from jax.sharding import PartitionSpec as P

CG_ITERS = 2


highest = lax.Precision.HIGHEST
norm_epsilon = 1e-05
beta_one = 0.9
beta_two = 0.999
adam_epsilon = 1e-08
decay_rate = 0.01
rate_conv = 0.04
rate_norm = 0.1
rate_penalty = 0.01


def for_sending(x):
    return jax.tree.map(lambda a: a.astype(jnp.bfloat16) if a.dtype == jnp.float32 else a, x)


def with_halo(x, sides, width):
    for axis, dim in sides:
        size, length = (lax.axis_size(axis), x.shape[dim])
        up = [(i, (i + 1) % size) for i in range(size - 1)]
        down = [(j, i) for i, j in up]
        last = lax.slice_in_dim(x, length - width, length, axis=dim)
        first = lax.slice_in_dim(x, 0, width, axis=dim)
        before = lax.ppermute(last, axis, up)
        after = lax.ppermute(first, axis, down)
        x = jnp.concatenate([before, x, after], axis=dim)
    return x


def dft_tables(length):
    index = jnp.arange(length, dtype=jnp.int32)
    phase = index[:, None] * index[None, :] % length
    angle = phase.astype(jnp.float32) * (2.0 * math.pi / length)
    factor = 1.0 / math.sqrt(length)
    return (jnp.cos(angle) * factor, jnp.sin(angle) * factor)


def cols_forward(values, table):
    return jnp.einsum("...hw,wv->...vh", values, table, precision=highest)


def rows_across(values, table):
    return jnp.einsum("...wk,kh->...wh", values, table, precision=highest)


def cols_back(values, table):
    return jnp.einsum("...vh,vw->...hw", values, table, precision=highest)


def rotate(real_part, imag_part, table_pair, multiply, orient):
    cosine, sine_table = table_pair
    return (
        multiply(real_part, cosine) + orient * multiply(imag_part, sine_table),
        multiply(imag_part, cosine) - orient * multiply(real_part, sine_table),
    )


def to_image(spec_real, spec_imag, coil_maps, tables):
    back_real, back_imag = rotate(spec_real, spec_imag, tables[1], rows_across, -1.0)
    rowwise = lax.all_to_all(
        jnp.stack([back_real, back_imag], 2), "img", split_axis=4, concat_axis=3, tiled=True
    )
    coil_real, coil_imag = rotate(rowwise[:, :, 0], rowwise[:, :, 1], tables[0], cols_back, -1.0)
    sens_real = coil_maps[:, :, 0]
    sens_imag = coil_maps[:, :, 1]
    return jnp.stack(
        [
            jnp.sum(sens_real * coil_real + sens_imag * coil_imag, 1),
            jnp.sum(sens_real * coil_imag - sens_imag * coil_real, 1),
        ],
        1,
    )


def normal_op(search, coil_maps, sample_field, penalty_value, tables):
    sens_real = coil_maps[:, :, 0]
    sens_imag = coil_maps[:, :, 1]
    field_real = search[:, 0][:, None]
    field_imag = search[:, 1][:, None]
    coil_real, coil_imag = rotate(
        sens_real * field_real - sens_imag * field_imag,
        sens_real * field_imag + sens_imag * field_real,
        tables[0],
        cols_forward,
        1.0,
    )
    columns = lax.all_to_all(
        for_sending(jnp.stack([coil_real, coil_imag], 2)),
        "img",
        split_axis=3,
        concat_axis=4,
        tiled=True,
    )
    spec_real, spec_imag = rotate(columns[:, :, 0], columns[:, :, 1], tables[1], rows_across, 1.0)
    sampled = sample_field[:, None]
    return (
        to_image(spec_real * sampled, spec_imag * sampled, coil_maps, tables)
        + penalty_value * search
    )


def adjoint_data(kspace_turned, coil_maps, sample_field, tables):
    sampled = sample_field[:, None]
    return to_image(
        kspace_turned[:, :, 0] * sampled, kspace_turned[:, :, 1] * sampled, coil_maps, tables
    )


def dot_images(left, right):
    return jnp.sum(left * right, axis=(1, 2, 3))


def widen(values):
    return values[:, None, None, None]


def image_sums(stacked):
    return lax.psum(stacked, "img")


def solve_forward(right_side, operator):
    iterate = jnp.zeros_like(right_side)
    residual = right_side
    search = right_side
    norm_now = image_sums(jnp.stack([dot_images(residual, residual)]))[0]
    saved = []
    for sweep in range(CG_ITERS):
        image = operator(search)
        curve = image_sums(jnp.stack([dot_images(search, image)]))[0]
        alpha = norm_now / curve
        iterate = iterate + widen(alpha) * search
        residual = residual - widen(alpha) * image
        norm_next = image_sums(jnp.stack([dot_images(residual, residual)]))[0]
        ratio = norm_next / norm_now
        saved.append((search, image, residual, norm_now, curve, alpha, ratio, norm_next))
        search = residual + widen(ratio) * search
        norm_now = norm_next
    return (iterate, saved)


def solve_backward(grad_out, saved, right_side, operator):
    grad_res = jnp.zeros_like(right_side)
    grad_search = jnp.zeros_like(right_side)
    grad_norm = jnp.zeros((right_side.shape[0],), jnp.float32)
    penalty_part = jnp.zeros((), jnp.float32)
    for entry in reversed(saved):
        search, image, residual, norm_now, curve, alpha, ratio, norm_next = entry
        sums = image_sums(
            jnp.stack(
                [
                    dot_images(grad_search, search),
                    dot_images(grad_out, search),
                    dot_images(grad_res, image),
                    dot_images(grad_search, image),
                    dot_images(residual, image),
                ]
            )
        )
        grad_next = grad_norm + sums[0] / norm_now
        grad_alpha = sums[1] - sums[2] - sums[3] - 2.0 * grad_next * sums[4]
        grad_total = grad_res + grad_search + 2.0 * widen(grad_next) * residual
        grad_curve = -grad_alpha * alpha / curve
        grad_image = widen(-alpha) * grad_total + widen(grad_curve) * search
        penalty_part = penalty_part + jnp.sum(grad_image * search)
        grad_search = (
            widen(ratio) * grad_search
            + widen(alpha) * grad_out
            + widen(grad_curve) * image
            + operator(grad_image)
        )
        grad_norm = -sums[0] * norm_next / (norm_now * norm_now) + grad_alpha / curve
        grad_res = grad_total
    return (grad_res + grad_search + 2.0 * widen(grad_norm) * right_side, penalty_part)


def rows_halo(values):
    return with_halo(values, (("img", 2),), 1)


def gather_images(values):
    return lax.all_gather(values, "ch", axis=1, tiled=True)


def images_scatter(values):
    return lax.psum_scatter(
        values.astype(jnp.bfloat16), "ch", scatter_dimension=1, tiled=True
    ).astype(jnp.float32)


def channels_full(values):
    return lax.all_gather(values, "ch", axis=0, tiled=True)


def widen_cols(padded):
    return jnp.pad(padded, ((0, 0), (0, 0), (0, 0), (1, 1)))


def conv_taps(padded, weight):
    row_count = padded.shape[2] - 2
    col_count = padded.shape[3]
    wide = widen_cols(padded)
    summed = jnp.zeros((weight.shape[1], padded.shape[1], row_count, col_count), jnp.float32)
    for row_shift in range(3):
        for col_shift in range(3):
            window = wide[
                :, :, row_shift : row_shift + row_count, col_shift : col_shift + col_count
            ]
            summed = summed + jnp.einsum(
                "oc,cnhw->onhw",
                weight[3 * row_shift + col_shift],
                window,
                preferred_element_type=jnp.float32,
            )
    return summed


def conv_input_grad(grad_padded, weight):
    row_count = grad_padded.shape[2] - 2
    col_count = grad_padded.shape[3]
    wide = widen_cols(grad_padded)
    summed = jnp.zeros((weight.shape[2], grad_padded.shape[1], row_count, col_count), jnp.float32)
    for row_shift in range(3):
        for col_shift in range(3):
            window = wide[
                :,
                :,
                2 - row_shift : 2 - row_shift + row_count,
                2 - col_shift : 2 - col_shift + col_count,
            ]
            summed = summed + jnp.einsum(
                "oc,onhw->cnhw",
                weight[3 * row_shift + col_shift],
                window,
                preferred_element_type=jnp.float32,
            )
    return summed


def conv_weight_grad(grad_low, padded):
    row_count = grad_low.shape[2]
    col_count = grad_low.shape[3]
    wide = widen_cols(padded)
    pieces = []
    for row_shift in range(3):
        for col_shift in range(3):
            window = wide[
                :, :, row_shift : row_shift + row_count, col_shift : col_shift + col_count
            ]
            pieces.append(
                jnp.einsum("onhw,cnhw->oc", grad_low, window, preferred_element_type=jnp.float32)
            )
    return jnp.stack(pieces)


def channel_sums(grad_padded, weight):
    return lax.psum_scatter(
        conv_input_grad(grad_padded, weight).astype(jnp.bfloat16),
        "ch",
        scatter_dimension=0,
        tiled=True,
    ).astype(jnp.float32)


def norm_forward(hidden, gain_bias, valid_field):
    weight_mask = valid_field[None]
    sum_first, sum_second, pixel_count = lax.psum(
        (
            jnp.sum(hidden * weight_mask, axis=(1, 2, 3)),
            jnp.sum(hidden * hidden * weight_mask, axis=(1, 2, 3)),
            jnp.sum(valid_field),
        ),
        "img",
    )
    average = sum_first / pixel_count
    scale_inv = lax.rsqrt(sum_second / pixel_count - average * average + norm_epsilon)
    normed = (hidden - widen(average)) * widen(scale_inv)
    shaped = widen(gain_bias[0]) * normed + widen(gain_bias[1])
    activation = jnp.maximum(shaped, 0.0).astype(jnp.bfloat16)
    return (activation, (normed, shaped > 0.0, scale_inv), pixel_count)


def norm_backward(grad_act, saved, gain_bias, valid_field, pixel_count):
    normed, positive, scale_inv = saved
    grad_shaped = jnp.where(positive, grad_act, 0.0)
    sum_plain, sum_normed = lax.psum(
        (jnp.sum(grad_shaped, axis=(1, 2, 3)), jnp.sum(grad_shaped * normed, axis=(1, 2, 3))), "img"
    )
    weight_mask = valid_field[None]
    grad_hidden = widen(gain_bias[0] * scale_inv) * (
        grad_shaped - weight_mask * (widen(sum_plain) + normed * widen(sum_normed)) / pixel_count
    )
    return (grad_hidden, sum_normed, sum_plain)


def denoise_forward(field, weights, norm_params, valid_field):
    first_low, middle_low, last_low, own_columns = weights
    images = gather_images(jnp.transpose(field.astype(jnp.bfloat16), (1, 0, 2, 3)))
    padded = rows_halo(images)
    hidden = conv_taps(padded, first_low)
    stored = [padded]
    normed = []
    for layer in range(4):
        activation, saved, pixel_count = norm_forward(hidden, norm_params[layer], valid_field)
        normed.append(saved)
        padded = rows_halo(activation)
        if layer < 3:
            gathered = channels_full(padded)
            hidden = conv_taps(gathered, middle_low[layer])
            stored.append(gathered)
        else:
            stored.append(padded)
            partial_sum = conv_taps(padded, last_low)
    branch = jnp.transpose(images_scatter(partial_sum), (1, 0, 2, 3))
    return (field + branch, (stored, normed), pixel_count)


def denoise_backward(grad_field, saved, weights, norm_params, valid_field, pixel_count):
    first_low, middle_low, last_low, own_columns = weights
    stored, normed = saved
    grad_images = gather_images(jnp.transpose(grad_field.astype(jnp.bfloat16), (1, 0, 2, 3)))
    grad_last = conv_weight_grad(grad_images, stored[4])
    grad_act = conv_input_grad(rows_halo(grad_images), last_low)
    grad_middle = [None, None, None]
    grad_norms = [None, None, None, None]
    grad_input = None
    grad_first = None
    for layer in (3, 2, 1, 0):
        grad_hidden, grad_gain, grad_bias = norm_backward(
            grad_act, normed[layer], norm_params[layer], valid_field, pixel_count
        )
        grad_norms[layer] = jnp.stack([grad_gain, grad_bias])
        grad_low = grad_hidden.astype(jnp.bfloat16)
        if layer > 0:
            gathered = stored[layer]
            grad_middle[layer - 1] = conv_weight_grad(grad_low, gathered)
            grad_act = channel_sums(rows_halo(grad_low), middle_low[layer - 1])
        else:
            grad_first = conv_weight_grad(grad_low, stored[0])
    return (grad_input, (grad_first, jnp.stack(grad_middle), grad_last, jnp.stack(grad_norms)))


def adamw(weight, grad, first_m, second_m, rate, decay, step_value):
    mean_new = beta_one * first_m + (1.0 - beta_one) * grad
    square_new = beta_two * second_m + (1.0 - beta_two) * grad * grad
    mean_hat = mean_new / (1.0 - beta_one**step_value)
    square_hat = square_new / (1.0 - beta_two**step_value)
    updated = weight - rate * (mean_hat / (jnp.sqrt(square_hat) + adam_epsilon) + decay * weight)
    return (updated, mean_new, square_new)


def body(
    kspace_data,
    coil_maps,
    sample_mask,
    valid_mask,
    target,
    first_weight,
    middle_weights,
    last_weight,
    norm_params,
    penalty,
    first_mean,
    first_square,
    middle_mean,
    middle_square,
    last_mean,
    last_square,
    norm_mean,
    norm_square,
    penalty_mean,
    penalty_square,
    step_count,
):
    tables = (dft_tables(coil_maps.shape[-1]), dft_tables(kspace_data.shape[3]))
    kspace_turned = jnp.transpose(kspace_data, (0, 1, 2, 4, 3))
    sample_field = jnp.transpose(sample_mask, (0, 2, 1)).astype(jnp.float32)
    valid_field = valid_mask.astype(jnp.float32)
    local_images = target.shape[0]
    valid_local = lax.dynamic_slice_in_dim(
        valid_field, lax.axis_index("ch") * local_images, local_images, 0
    )
    penalty_value = penalty[0]
    middle_low = middle_weights.astype(jnp.bfloat16)
    weights = (
        first_weight.astype(jnp.bfloat16),
        middle_low,
        last_weight.astype(jnp.bfloat16),
        middle_low,
    )

    def operator(search):
        return normal_op(search, coil_maps, sample_field, penalty_value, tables)

    initial = adjoint_data(kspace_turned, coil_maps, sample_field, tables)
    field = initial
    denoised, kept, pixel_count = denoise_forward(field, weights, norm_params, valid_field)
    right_side = initial + penalty_value * denoised
    field, solver_saved = solve_forward(right_side, operator)
    history = (denoised, kept, right_side, solver_saved)
    difference = field - target
    mask_local = valid_local[:, None]
    loss_part = jnp.sum(mask_local * difference * difference) / pixel_count
    grad_field = 2.0 * mask_local * difference / pixel_count
    penalty_part = jnp.zeros((), jnp.float32)
    denoised, kept, right_side, solver_saved = history
    grad_right, solver_penalty = solve_backward(grad_field, solver_saved, right_side, operator)
    penalty_part = penalty_part + solver_penalty + jnp.sum(grad_right * denoised)
    grad_input, layer_grads = denoise_backward(
        penalty_value * grad_right, kept, weights, norm_params, valid_field, pixel_count
    )
    grad_first, grad_middle, grad_last = lax.psum(
        (layer_grads[0], layer_grads[1], layer_grads[2]), "img"
    )
    loss_value, grad_penalty = lax.psum((loss_part, penalty_part), ("img", "ch"))
    step_value = step_count[0].astype(jnp.float32) + 1.0
    first_new, first_mean_new, first_square_new = adamw(
        first_weight, grad_first, first_mean, first_square, rate_conv, decay_rate, step_value
    )
    middle_new, middle_mean_new, middle_square_new = adamw(
        middle_weights, grad_middle, middle_mean, middle_square, rate_conv, decay_rate, step_value
    )
    last_new, last_mean_new, last_square_new = adamw(
        last_weight, grad_last, last_mean, last_square, rate_conv, decay_rate, step_value
    )
    norm_new, norm_mean_new, norm_square_new = adamw(
        norm_params, layer_grads[3], norm_mean, norm_square, rate_norm, 0.0, step_value
    )
    penalty_new, penalty_mean_new, penalty_square_new = adamw(
        penalty, grad_penalty[None], penalty_mean, penalty_square, rate_penalty, 0.0, step_value
    )
    penalty_state = jnp.concatenate([penalty_new, penalty_mean_new, penalty_square_new])
    return (
        loss_value,
        first_new,
        first_mean_new,
        first_square_new,
        middle_new,
        middle_mean_new,
        middle_square_new,
        last_new,
        last_mean_new,
        last_square_new,
        norm_new,
        norm_mean_new,
        norm_square_new,
        penalty_state,
    )


def solution(mesh):
    in_specs = (
        P("ch", None, None, None, "img"),
        P("ch", None, None, "img", None),
        P("ch", None, "img"),
        P(None, "img", None),
        P("ch", None, "img", None),
        P(None, "ch", None),
        P(None, None, "ch", None),
        P(None, None, "ch"),
        P(None, None, "ch"),
        P(),
        P(None, "ch", None),
        P(None, "ch", None),
        P(None, None, "ch", None),
        P(None, None, "ch", None),
        P(None, None, "ch"),
        P(None, None, "ch"),
        P(None, None, "ch"),
        P(None, None, "ch"),
        P(),
        P(),
        P(),
    )
    out_specs = (
        P(),
        P(None, "ch", None),
        P(None, "ch", None),
        P(None, "ch", None),
        P(None, None, "ch", None),
        P(None, None, "ch", None),
        P(None, None, "ch", None),
        P(None, None, "ch"),
        P(None, None, "ch"),
        P(None, None, "ch"),
        P(None, None, "ch"),
        P(None, None, "ch"),
        P(None, None, "ch"),
        P(),
    )
    return jax.shard_map(body, mesh=mesh, in_specs=in_specs, out_specs=out_specs, check_vma=False)
```

profile of v0, /device:TPU:0, one launch (start us, length us, event | category | flops | bytes accessed | tf_op | source)
XLA Modules:
  0.0 2238.9 jit_solution(5117604724643340184)
XLA Ops:
  55.3 28.3 %all-to-all-done = f32[8,1,38400]{2,1,0:T(1,128)S(1)} async-done(((f32[8,1,38400]{2,1,0:T(1,128)}), f32[8,1,38400]{2,1,0:T(1,128)S(1)}, u32[]{:S(2)}, u32[]{:S(2)}) %all-to-all-start) | async-done | bytes 1228832 | tf_op jit(solution)/shard_map/all_to_all | solution.py:69
  195.6 54.8 %all-gather.5.cloned.1.call-done = bf16[64,4,42,320]{3,0,2,1:T(8,128)(2,1)} async-done(((bf16[16,4,42,320]{3,0,2,1:T(8,128)(2,1)}), bf16[64,4,42,320]{3,0,2,1:T(8,128)(2,1)}) %all-gather.5.cloned.1.call-update) | async-done | bytes 6881296 | tf_op jit(solution)/shard_map/all_gather | solution.py:200
  298.9 21.5 all-reduce.18
  333.8 55.2 %all-gather.7.cloned.1.call-done = bf16[64,4,42,320]{3,0,2,1:T(8,128)(2,1)} async-done(((bf16[16,4,42,320]{3,0,2,1:T(8,128)(2,1)}), bf16[64,4,42,320]{3,0,2,1:T(8,128)(2,1)}) %all-gather.7.cloned.1.call-update) | async-done | bytes 6881296 | tf_op jit(solution)/shard_map/all_gather | solution.py:200
  437.2 21.8 all-reduce.17
  472.3 55.1 %all-gather.9.cloned.1.call-done = bf16[64,4,42,320]{3,0,2,1:T(8,128)(2,1)} async-done(((bf16[16,4,42,320]{3,0,2,1:T(8,128)(2,1)}), bf16[64,4,42,320]{3,0,2,1:T(8,128)(2,1)}) %all-gather.9.cloned.1.call-update) | async-done | bytes 6881296 | tf_op jit(solution)/shard_map/all_gather | solution.py:200
  575.9 21.4 all-reduce.16
  653.3 22.4 all_to_all.162
  722.9 32.6 %all_to_all.163 = f32[8,1,38400]{2,1,0:T(1,128)} all-to-all(f32[8,1,38400]{2,1,0:T(1,128)S(1)} %reshape.2604), channel_id=1, replica_groups=mesh['img'=8,'ch'=4] {'img'}, dimensions={0} | all-to-all | bytes 2457600 | tf_op jit(solution)/shard_map/all_to_all | solution.py:69
  793.7 19.9 all-reduce.15
  925.4 21.2 all-to-all-done.4
  984.6 19.9 psum.224
  1127.3 26.0 %psum.227 = f32[1]{0:T(128)} all-reduce(f32[1]{0:T(128)} %bitcast.222), channel_id=1, replica_groups=mesh['img'=8,'ch'=4] {'img'}, use_global_device_ids=true, to_apply=%region_41.42 | all-reduce | flops 1 | bytes 8 | tf_op jit(solution)/shard_map/psum | solution.py:127
  1412.8 19.9 all-reduce.14
  1507.6 42.5 %fusion = bf16[64,4,40,320]{3,0,2,1:T(8,128)(2,1)} fusion(f32[4,40,320,64]{2,3,1,0:T(8,128)} %fusion.108, f32[4,40,320,64]{2,3,1,0:T(8,128)} %fusion.160, f32[4,40,320,64]{2,3,1,0:T(8,128)} %fusion.162, f32[4,40,320,64]{2,3,1,0:T(8,128)} %fusion.740, f32[4,40,320,64]{2,3,1,0:T(8,128)} %fusion.164, f32[4,40,320,64]{2,3,1,0:T(8,128)} %fusion.166, ...), kind=kOutput, calls=%fused_computation.3 | convolution fusion | flops 134348800 | bytes 113381376 | tf_op jit(solution)/shard_map/oc,onhw->cnhw/dot_general | solution.py:239
  1550.3 53.9 %pad_slice_fusion.12 = (bf16[64,4,40,320]{3,0,2,1:T(8,128)(2,1)}, bf16[64,4,40,320]{3,0,2,1:T(8,128)(2,1)}, bf16[64,4,40,320]{3,0,2,1:T(8,128)(2,1)}, bf16[64,4,...) fusion(bf16[64,4,42,320]{3,0,2,1:T(8,128)(2,1)} %all-gather.5.c, ...), kind=kLoop, calls=%fused_computation.154 | loop fusion | bytes 90832896 | tf_op jit(solution)/shard_map/slice | solution.py:214
  1604.2 53.8 %pad_slice_fusion.6 = (bf16[64,4,40,320]{3,0,2,1:T(8,128)(2,1)}, bf16[64,4,40,320]{3,0,2,1:T(8,128)(2,1)}, bf16[64,4,40,320]{3,0,2,1:T(8,128)(2,1)}, bf16[64,4,4...) fusion(bf16[64,4,42,320]{3,0,2,1:T(8,128)(2,1)} %all-gather.7.c, ...), kind=kLoop, calls=%fused_computation.148 | loop fusion | bytes 90832896 | tf_op jit(solution)/shard_map/slice | solution.py:214
  1754.7 42.4 %fusion.1 = bf16[64,4,40,320]{3,0,2,1:T(8,128)(2,1)} fusion(f32[4,40,320,64]{2,3,1,0:T(8,128)} %fusion.116, f32[4,40,320,64]{2,3,1,0:T(8,128)} %fusion.146, f32[4,40,320,64]{2,3,1,0:T(8,128)} %fusion.148, f32[4,40,320,64]{2,3,1,0:T(8,128)} %fusion.732, f32[4,40,320,64]{2,3,1,0:T(8,128)} %fusion.150, f32[4,40,320,64]{2,3,1,0:T(8,128)} %fusion.152, ...), kind=kOutput, calls=%fused_computation.4 | convolution fusion | flops 134348800 | bytes 113381376 | tf_op jit(solution)/shard_map/oc,onhw->cnhw/dot_general | solution.py:239
  1797.2 52.6 %pad_slice_fusion = (bf16[64,4,40,320]{3,0,2,1:T(8,128)(2,1)S(1)}, bf16[64,4,40,320]{3,0,2,1:T(8,128)(2,1)}, bf16[64,4,40,320]{3,0,2,1:T(8,128)(2,1)}, bf16[64,4...) fusion(bf16[64,4,42,320]{3,0,2,1:T(8,128)(2,1)} %all-gather.9.c, ...), kind=kLoop, calls=%fused_computation.142 | loop fusion | bytes 90832896 | tf_op jit(solution)/shard_map/slice | solution.py:214
  1917.7 19.4 all-reduce.12
  2045.9 42.4 %fusion.2 = bf16[64,4,40,320]{3,0,2,1:T(8,128)(2,1)} fusion(f32[4,40,320,64]{2,3,1,0:T(8,128)} %fusion.124, f32[4,40,320,64]{2,3,1,0:T(8,128)} %fusion.132, f32[4,40,320,64]{2,3,1,0:T(8,128)} %fusion.134, f32[4,40,320,64]{2,3,1,0:T(8,128)} %fusion.724, f32[4,40,320,64]{2,3,1,0:T(8,128)} %fusion.136, f32[4,40,320,64]{2,3,1,0:T(8,128)} %fusion.138, ...), kind=kOutput, calls=%fused_computation.5 | convolution fusion | flops 134348800 | bytes 134352896 | tf_op jit(solution)/shard_map/oc,onhw->cnhw/dot_general | solution.py:239
  2105.7 38.6 %all-reduce.9 = (f32[]{:T(128)}, f32[1]{0:T(128)}) all-reduce(f32[]{:T(128)S(6)} %div.170, f32[1]{0:T(128)} %bitcast.509), channel_id=1, replica_groups=mesh['img'=8,'ch'=4] {'img','ch'}, use_global_device_ids=true, to_apply=%region_34.35 | all-reduce | flops 2 | bytes 16 | tf_op jit(solution)/shard_map/psum | solution.py:423
  2164.4 20.8 all-reduce.11
  2196.9 33.0 %all-reduce.10 = (f32[9,16,2]{1,2,0:T(2,128)S(1)}, f32[9,2,16]{2,1,0:T(2,128)S(1)}) all-reduce(f32[9,16,2]{1,2,0:T(2,128)S(1)} %fusion.466, f32[9,2,16]{2,1,0:T(2,128)S(1)} %fusion.463), channel_id=1, replica_groups=mesh['img'=8,'ch'=4] {'img'}, use_global_device_ids=true, to_apply=%region_71.72 | all-reduce | flops 576 | bytes 4608 | tf_op jit(solution)/shard_map/psum | solution.py:420
  (763 shorter events, 1373.0 us)
Async XLA Ops:
  46.7 36.9 %all-to-all-start = ((f32[8,1,38400]{2,1,0:T(1,128)}), f32[8,1,38400]{2,1,0:T(1,128)S(1)}, u32[]{:S(2)}, u32[]{:S(2)}) async-start(f32[8,1,38400]{2,1,0:T(1,128)} %reshape.2600), calls=%async_computation | async-start | bytes 2457600 | tf_op jit(solution)/shard_map/all_to_all | solution.py:69
  54.0 196.4 %all-gather.5.cloned.1.call-start = ((), (), s32[]{:S(2)}) async-start(), calls=%async_computation.13 | async-start | bytes 10321920 | tf_op jit(solution)/shard_map/all_gather | solution.py:200
  187.3 6.0 collective-permute-start.3
  195.1 193.8 %all-gather.7.cloned.1.call-start = ((), (), s32[]{:S(2)}) async-start(), calls=%async_computation.14 | async-start | bytes 10321920 | tf_op jit(solution)/shard_map/all_gather | solution.py:200
  325.9 6.0 collective-permute-start.5
  333.7 193.8 %all-gather.9.cloned.1.call-start = ((), (), s32[]{:S(2)}) async-start(), calls=%async_computation.15 | async-start | bytes 10321920 | tf_op jit(solution)/shard_map/all_gather | solution.py:200
  464.5 6.0 collective-permute-start.7
  472.3 160.9 %reduce-scatter.5.cloned.1.call-start = ((), (), s32[]{:S(2)}) async-start(), calls=%async_computation.16 | async-start | bytes 307200 | tf_op jit(solution)/shard_map/reduce_scatter | solution.py:194
  602.2 6.0 collective-permute-start.9
  921.1 25.5 %all-to-all-start.4 = ((f32[8,1,38400]{2,1,0:T(1,128)}), f32[8,1,38400]{2,1,0:T(1,128)}, u32[]{:S(2)}, u32[]{:S(2)}) async-start(f32[8,1,38400]{2,1,0:T(1,128)} %reshape.2608), calls=%async_computation.5 | async-start | bytes 2457600 | tf_op jit(solution)/shard_map/all_to_all | solution.py:69
  1121.7 34.9 %all-to-all-start.6 = ((f32[8,1,38400]{2,1,0:T(1,128)}), f32[8,1,38400]{2,1,0:T(1,128)}, u32[]{:S(2)}, u32[]{:S(2)}) async-start(f32[8,1,38400]{2,1,0:T(1,128)} %reshape.2612), calls=%async_computation.7 | async-start | bytes 2457600 | tf_op jit(solution)/shard_map/all_to_all | solution.py:69
  1310.1 22.6 %all-to-all-start.8 = ((f32[8,1,38400]{2,1,0:T(1,128)}), f32[8,1,38400]{2,1,0:T(1,128)}, u32[]{:S(2)}, u32[]{:S(2)}) async-start(f32[8,1,38400]{2,1,0:T(1,128)} %reshape.2616), calls=%async_computation.9 | async-start | bytes 2457600 | tf_op jit(solution)/shard_map/all_to_all | solution.py:69
  1314.4 343.7 %reduce-scatter.7.cloned.1.call-start = ((), (), s32[]{:S(2)}) async-start(), calls=%async_computation.17 | async-start | bytes 9830400 | tf_op jit(solution)/shard_map/reduce_scatter | solution.py:265
  1377.4 6.6 collective-permute-start.11
  1378.7 5.9 collective-permute-start.10
  1438.0 13.9 collective-permute-start.13
  1439.3 12.6 collective-permute-start.12
  1550.1 362.8 %reduce-scatter.9.cloned.1.call-start = ((), (), s32[]{:S(2)}) async-start(), calls=%async_computation.18 | async-start | bytes 9830400 | tf_op jit(solution)/shard_map/reduce_scatter | solution.py:265
  1685.0 14.0 collective-permute-start.15
  1686.3 12.7 collective-permute-start.14
  1797.1 360.5 %all-reduce.22.cloned.1.call-start = ((), (), s32[]{:S(2)}) async-start(), calls=%async_computation.20 | async-start | bytes 442368 | tf_op jit(solution)/shard_map/psum | solution.py:420
  1950.7 33.2 %collective-permute-start.17 = (bf16[16,4,1,320]{3,0,2,1:T(8,128)(2,1)S(1)}, bf16[16,4,1,320]{3,0,2,1:T(8,128)(2,1)S(1)}, u32[]{:S(2)}, u32[]{:S(2)}) collective-permute-start(bf16[16,4,1,320]{3,0,2,1:T(8,128)(2,1)S(1)} %get-tuple-element.153), channel_id=1, source_target_pairs={{4,0},{8,4},{12,8},{16,12},{20,16},{24,20},{28,24},{5,1},{9,5},{13... | collective-permute-start | bytes 122888 | tf_op jit(solution)/shard_map/ppermute | solution.py:34
  1952.0 31.9 %collective-permute-start.16 = (bf16[16,4,1,320]{3,0,2,1:T(8,128)(2,1)S(1)}, bf16[16,4,1,320]{3,0,2,1:T(8,128)(2,1)S(1)}, u32[]{:S(2)}, u32[]{:S(2)}) collective-permute-start(bf16[16,4,1,320]{3,0,2,1:T(8,128)(2,1)S(1)} %get-tuple-element.154), channel_id=1, source_target_pairs={{0,4},{4,8},{8,12},{12,16},{16,20},{20,24},{24,28},{1,5},{5,9},{9,... | collective-permute-start | bytes 122888 | tf_op jit(solution)/shard_map/ppermute | solution.py:33
  1983.6 175.9 %reduce-scatter.11.cloned.1.call-start = ((), (), s32[]{:S(2)}) async-start(), calls=%async_computation.19 | async-start | bytes 9830400 | tf_op jit(solution)/shard_map/reduce_scatter | solution.py:265
  (174 other events, 5914.7 us)
Sparse Core Ops, SparseCore 0:
  195.3 55.1 all-gather.4
  333.8 55.0 all-gather.6
  472.4 55.0 all-gather.8
  615.6 17.4 reduce-scatter.4
  1550.2 65.3 reduce-scatter.6
  1797.2 67.3 reduce-scatter.8
  1983.7 66.7 all-reduce.21
  2088.5 66.8 reduce-scatter.10
where the time goes:
time: 2250 us; the launch traced here: 2240 us
  matrix products  882 us (39%)
  blocking collectives  464 us (21%)
  local copies, waits for them, and re-layouts  406 us (18%)
  waiting for transfers between devices  269 us (12%)
  other arithmetic  110 us (5%)
  starting transfers between devices  62.6 us (3%)
  between operations  46.4 us (2%)
    dot_general x36, matrix products, conv_input_grad(): jnp.einsum('oc,onhw->cnhw', weight[3 * row_shift + col_shift], window, pr...  347 us
    dot_general x45, matrix products, conv_taps(): jnp.einsum('oc,cnhw->onhw', weight[3 * row_shift + col_shift], window, pr...  176 us
    slice x5, local copies, waits for them, and re-layouts, conv_taps(): wide[:, :, row_shift:row_shift + row_count, col_shift:col_shift + col_count]  169 us
    all_gather x3, waiting for transfers between devices, channels_full(): return lax.all_gather(values, 'ch', axis=0, tiled=True)  165 us
    dot_general x36, matrix products, rows_across(): return jnp.einsum('...wk,kh->...wh', values, table, precision=highest)  123 us
    unnamed x356, local copies, waits for them, and re-layouts  121 us
    psum x6, blocking collectives, image_sums(): return lax.psum(stacked, 'img')  120 us
    dot_general x45, matrix products, conv_weight_grad(): jnp.einsum('onhw,cnhw->oc', grad_low, window, preferred_element_type=jnp....  105 us
  transfers between devices with their start and end apart: 30, of which 16 were waited for; matrix products, arithmetic and copies ran while one was open for 18% of the time, Pallas kernels for 0%

commit v1 on v0

v1 whole, which is shorter than its diff:
```python
import math

import jax
import jax.numpy as jnp
import numpy as np
from jax import lax
from jax.experimental import pallas as pl
from jax.experimental.pallas import tpu as pltpu
from jax.sharding import PartitionSpec as P

norm_epsilon = 1e-05
beta_one = 0.9
beta_two = 0.999
adam_epsilon = 1e-08
decay_rate = 0.01
rate_conv = 0.04
rate_norm = 0.1
rate_penalty = 0.01

BOTH = ("img", "ch")
f32 = jnp.float32
bf16 = jnp.bfloat16
CH = 64
LANES = 384
HALO = 7


def rup(n, m):
    return (n + m - 1) // m * m


def params():
    return pltpu.CompilerParams(vmem_limit_bytes=60 * 1024 * 1024)


def call(kernel, outs, *args, scratch=(), name=None):
    return pl.pallas_call(
        kernel,
        out_shape=[jax.ShapeDtypeStruct(s, d) for s, d in outs],
        scratch_shapes=list(scratch),
        compiler_params=params(),
        name=name,
    )(*args)


def dft_tables(n):
    k = np.arange(n)
    angle = (k[:, None] * k[None, :] % n) * (2.0 * math.pi / n)
    cosine = np.cos(angle) / math.sqrt(n)
    sine = np.sin(angle) / math.sqrt(n)
    right_forward = np.block([[cosine, -sine], [sine, cosine]])
    right_back = np.block([[cosine, sine], [-sine, cosine]])
    left = np.concatenate([cosine, sine], 0)
    return tuple(jnp.asarray(t.astype(np.float32)).astype(bf16) for t in (right_forward, right_back, left))


def swap(values):
    return pltpu.roll(values, values.shape[-1] // 2, values.ndim - 1)


def first_half(shape):
    return lax.broadcasted_iota(jnp.int32, shape, len(shape) - 1) < shape[-1] // 2


def mm(a, b):
    return jnp.dot(a, b, preferred_element_type=f32)


def left_dft(left, values, inverse):
    rows = left.shape[0] // 2
    both = mm(left, values)
    plain, crossed = both[:rows], swap(both[rows:])
    half = first_half(plain.shape)
    crossed = jnp.where(half, crossed, -crossed)
    return plain - crossed if inverse else plain + crossed


def map_pair(cat):
    half = first_half(cat.shape)
    other = swap(cat)
    return jnp.where(half, cat, other), jnp.where(half, -other, cat)


def spec_rows_kernel(kspace, mask, left, out, gathered):
    coils, _, _, cols = kspace.shape
    wide = gathered.shape[1] // 2
    gathered[...] = jnp.zeros(gathered.shape, f32)
    m = mask[...].astype(f32)
    for part in range(2):
        for coil in range(coils):
            gathered[:, part * wide + coil * cols : part * wide + (coil + 1) * cols] = kspace[coil, part] * m
    out[...] = left_dft(left[...], gathered[...].astype(bf16), True).astype(bf16)


def initial_kernel(spec, maps, right_back, out, gathered, cat):
    sources, rows, wide2 = spec.shape
    coils = maps.shape[0]
    wide = wide2 // 2
    width = maps.shape[3]
    cols = width // sources
    stride = gathered.shape[0] // coils
    if stride > rows:
        gathered[...] = jnp.zeros(gathered.shape, f32)
    for s in range(sources):
        block = spec[s].astype(f32)
        for part in range(2):
            for coil in range(coils):
                at = part * wide + coil * cols
                to = part * width + s * cols
                gathered[coil * stride : coil * stride + rows, to : to + cols] = block[:, at : at + cols]
    full = mm(gathered[...].astype(bf16), right_back[...])
    total = jnp.zeros((rows, 2 * width), f32)
    for coil in range(coils):
        cat[:, :width] = maps[coil, 0]
        cat[:, width:] = maps[coil, 1]
        real, imag = map_pair(cat[...])
        values = full[coil * stride : coil * stride + rows]
        total = total + real * values - imag * swap(values)
    out[...] = total


def apply_coils(vector, maps, mask2, right_forward, right_back, left):
    total = jnp.zeros(vector.shape, f32)
    other = swap(vector)
    for coil in range(maps.shape[0]):
        real, imag = map_pair(maps[coil].astype(f32))
        sent = (real * vector + imag * other).astype(bf16)
        step = mm(sent, right_forward[...]).astype(bf16)
        step = left_dft(left[...], step, False) * mask2
        step = left_dft(left[...], step.astype(bf16), True).astype(bf16)
        step = mm(step, right_back[...])
        total = total + real * step - imag * swap(step)
    return total


def dot_all(a, b):
    return jnp.sum(a * b)


def solve_first_kernel(right, maps, mask2, right_forward, right_back, left, out):
    vector = right[...].astype(f32)
    out[...] = apply_coils(vector, maps, mask2[...], right_forward, right_back, left).astype(bf16)


def first_step(right, applied, penalty):
    b = right.astype(f32)
    q0 = applied.astype(f32) + penalty * b
    rr0 = dot_all(b, b)
    pq0 = dot_all(b, q0)
    alpha0 = rr0 / pq0
    r1 = b - alpha0 * q0
    rn0 = dot_all(r1, r1)
    ratio0 = rn0 / rr0
    p1 = r1 + ratio0 * b
    return b, q0, rr0, pq0, alpha0, r1, rn0, ratio0, p1


def solve_second_kernel(right, applied0, maps, mask2, penalty, right_forward, right_back, left, out):
    p1 = first_step(right[...], applied0[...], penalty[0])[-1]
    out[...] = apply_coils(p1, maps, mask2[...], right_forward, right_back, left).astype(bf16)


def solve_back_kernel(
    right, applied0, applied1, maps, mask2, target, valid2, penalty, count,
    right_forward, right_back, left, out, rest, scalars
):
    lam = penalty[0]
    b, q0, rr0, pq0, alpha0, r1, rn0, ratio0, p1 = first_step(
        right[...], applied0[...], lam
    )
    q1 = applied1[...].astype(f32) + lam * p1
    pq1 = dot_all(p1, q1)
    alpha1 = rn0 / pq1
    x = alpha0 * b + alpha1 * p1
    difference = valid2[...] * (x - target[...])
    loss = dot_all(difference, difference) / count[0]
    gx = difference * (2.0 / count[0])
    ga1 = dot_all(gx, p1)
    gpq1 = -ga1 * alpha1 / pq1
    gp = alpha1 * gx + (2.0 * gpq1) * q1
    pen = gpq1 * dot_all(p1, p1)
    grr1 = ga1 / pq1
    d1 = dot_all(gp, b)
    d2 = dot_all(gx, b)
    d4 = dot_all(gp, q0)
    d5 = dot_all(r1, q0)
    grn = grr1 + d1 / rr0
    ga = d2 - d4 - 2.0 * grn * d5
    gr = gp + (2.0 * grn) * r1
    gpq = -ga * alpha0 / pq0
    gq = gpq * b - alpha0 * gr
    grr = ga / pq0 - d1 * rn0 / (rr0 * rr0)
    pen = pen + dot_all(gq, b)
    rest[...] = gr + ratio0 * gp + alpha0 * gx + gpq * q0 + (2.0 * grr) * b + lam * gq
    out[...] = apply_coils(gq, maps, mask2[...], right_forward, right_back, left).astype(bf16)
    lane = lax.broadcasted_iota(jnp.int32, scalars.shape, 1)
    scalars[...] = jnp.where(lane == 0, loss, jnp.where(lane == 1, pen, 0.0))


def per_channel(row):
    turned = jnp.transpose(jnp.broadcast_to(row, (128, 128)))
    tiled = jnp.concatenate([turned] * (LANES // 128), axis=1)
    return tiled[:CH], tiled[CH:]


def gathered_sums(stats):
    values = stats[...]
    row = lax.broadcasted_iota(jnp.int32, values.shape, 0) % 2
    sums = jnp.sum(jnp.where(row == 0, values, 0.0), axis=0, keepdims=True)
    counts = jnp.sum(jnp.where(row == 1, values, 0.0), axis=0, keepdims=True)
    return sums, counts[:, :1]


def norm_terms(stats, gain_bias):
    sums, count = gathered_sums(stats)
    means = sums / count
    average, second = per_channel(means)
    rstd = lax.rsqrt(second - average * average + norm_epsilon)
    gain, bias = per_channel(gain_bias[...])
    return average, rstd, gain, bias


def fold(values):
    return sum(values[:, 128 * t : 128 * (t + 1)] for t in range(LANES // 128))


def loop(count, step, carry):
    unroll = 2 if count % 2 == 0 else 1

    def several(t, state):
        for u in range(unroll):
            state = step(t * unroll + u, state)
        return state

    return lax.fori_loop(0, count // unroll, several, carry)


def write_sums(out, acc1, acc2, extra):
    both = jnp.concatenate([acc1, acc2], axis=0)
    row = jnp.sum(jnp.transpose(both), axis=0, keepdims=True)
    second = jnp.broadcast_to(extra, row.shape)
    which = lax.broadcasted_iota(jnp.int32, out.shape, 0) % 2
    out[...] = jnp.where(which == 0, row, second)


def conv_row(weight, stacked):
    y = mm(weight, stacked)
    n = y.shape[0] // 3
    return pltpu.roll(y[:n], 1, 1) + y[n : 2 * n] + pltpu.roll(y[2 * n :], LANES - 1, 1)


def first_conv_kernel(stacked, weight, mask, count, hidden, sums):
    w = weight[...]

    def row(r, acc):
        out = conv_row(w, stacked[r])
        hidden[r] = out
        kept = out * mask[pl.ds(r, 1), :]
        return acc[0] + fold(kept), acc[1] + fold(kept * out)

    zero = jnp.zeros((CH, 128), f32)
    acc = loop(hidden.shape[0], row, (zero, zero))
    write_sums(sums, *acc, count[0])


def conv_kernel(hidden, stats, gain_bias, weight, inside, mask, count, act, out, sums):
    average, rstd, gain, bias = norm_terms(stats, gain_bias)
    scale = gain * rstd
    shift = bias - average * scale
    w = weight[...]

    def activate(r):
        act[r] = (jnp.maximum(hidden[r] * scale + shift, 0.0) * inside[pl.ds(r, 1), :]).astype(bf16)

    activate(0)
    activate(1)

    def row(r, acc):
        activate(r + 2)
        value = conv_row(w, act[pl.ds(r, 3)].reshape(3 * CH, LANES))
        out[r] = value
        kept = value * mask[pl.ds(r, 1), :]
        return acc[0] + fold(kept), acc[1] + fold(kept * value)

    zero = jnp.zeros((CH, 128), f32)
    acc = loop(out.shape[0], row, (zero, zero))
    write_sums(sums, *acc, count[0])


def last_conv_kernel(hidden, stats, gain_bias, weight, inside, act, out, *, skip):
    average, rstd, gain, bias = norm_terms(stats, gain_bias)
    scale = gain * rstd
    shift = bias - average * scale
    w = weight[...]

    def activate(r):
        act[r] = (jnp.maximum(hidden[r + skip] * scale + shift, 0.0) * inside[pl.ds(r + skip, 1), :]).astype(bf16)

    activate(0)
    activate(1)

    def row(r, carry):
        activate(r + 2)
        out[r] = conv_row(w, act[pl.ds(r, 3)].reshape(3 * CH, LANES))
        return carry

    loop(out.shape[0], row, 0)


def grad_tail(ga, hidden_row, terms, inside_row):
    average, rstd, gain, bias = terms
    normed = (hidden_row - average) * rstd
    keep = (gain * normed + bias > 0.0) & (inside_row > 0.0)
    return jnp.where(keep, ga, 0.0), normed


def back_last_kernel(stacked, weight, hidden, stats, gain_bias, inside, own, gy, sums):
    terms = norm_terms(stats, gain_bias)
    w = weight[...]

    def row(r, acc):
        value, normed = grad_tail(conv_row(w, stacked[r]), hidden[r], terms, inside[pl.ds(r, 1), :])
        gy[r] = value
        kept = value * own[pl.ds(r, 1), :]
        return acc[0] + fold(kept), acc[1] + fold(kept * normed)

    zero = jnp.zeros((CH, 128), f32)
    acc = loop(gy.shape[0], row, (zero, zero))
    write_sums(sums, *acc, 0.0)


def hidden_grad_terms(stats, back_stats, gain_bias):
    average, rstd, gain, _ = norm_terms(stats, gain_bias)
    _, count = gathered_sums(stats)
    back, _ = gathered_sums(back_stats)
    s1, s2 = per_channel(back / count)
    return average, rstd, gain * rstd, s1, s2


def back_kernel(
    gy_in, hidden_in, stats_in, back_stats, gain_bias_in, mask,
    weight, hidden, stats, gain_bias, inside, own, grad, gy, sums, *, skip_in, skip
):
    average, rstd, scale, s1, s2 = hidden_grad_terms(stats_in, back_stats, gain_bias_in)
    terms = norm_terms(stats, gain_bias)
    w = weight[...]

    def hidden_grad(r):
        normed = (hidden_in[r + skip_in] - average) * rstd
        grad[r] = (scale * (gy_in[r] - mask[pl.ds(r, 1), :] * (s1 + normed * s2))).astype(bf16)

    hidden_grad(0)
    hidden_grad(1)

    def row(r, acc):
        hidden_grad(r + 2)
        ga = conv_row(w, grad[pl.ds(r, 3)].reshape(3 * CH, LANES))
        value, normed = grad_tail(ga, hidden[r + skip], terms, inside[pl.ds(r + skip, 1), :])
        gy[r] = value
        kept = value * own[pl.ds(r, 1), :]
        return acc[0] + fold(kept), acc[1] + fold(kept * normed)

    zero = jnp.zeros((CH, 128), f32)
    acc = loop(gy.shape[0], row, (zero, zero))
    write_sums(sums, *acc, 0.0)


def shifted(row):
    wide = row.astype(f32)
    return jnp.concatenate(
        [pltpu.roll(wide, LANES - 1, 1).astype(bf16), row.astype(bf16), pltpu.roll(wide, 1, 1).astype(bf16)], axis=0
    )


def outer(a, b):
    return lax.dot_general(a, b, (((1,), (1,)), ((), ())), preferred_element_type=f32)


def weight_grad_kernel(grad, act, out, *, rows, grad_skip, act_skip, stacked):
    step = 2 if rows % 2 == 0 else 1

    def block(t, carry):
        left = []
        right = []
        for u in range(step):
            r = t * step + u
            left.append(shifted(grad[r + grad_skip]))
            if stacked:
                right.append(act[r + act_skip])
            else:
                right.append(act[pl.ds(r + act_skip, 3)].reshape(-1, LANES))
        out[...] += outer(jnp.concatenate(left, axis=1), jnp.concatenate(right, axis=1))
        return carry

    out[...] = jnp.zeros(out.shape, f32)
    lax.fori_loop(0, rows // step, block, 0)


def first_back_kernel(gy_in, hidden_in, stats_in, back_stats, gain_bias_in, mask, stacked, out, *, hidden_skip, stack_skip):
    average, rstd, scale, s1, s2 = hidden_grad_terms(stats_in, back_stats, gain_bias_in)

    def row(r, carry):
        normed = (hidden_in[r + hidden_skip] - average) * rstd
        grad = scale * (gy_in[r] - mask[pl.ds(r, 1), :] * (s1 + normed * s2))
        out[...] += outer(shifted(grad), stacked[r + stack_skip])
        return carry

    out[...] = jnp.zeros(out.shape, f32)
    loop(gy_in.shape[0], row, 0)


def spread(values, axes, size):
    wide = jnp.broadcast_to(values[None], (size,) + values.shape).reshape((size * values.shape[0],) + values.shape[1:])
    return lax.all_to_all(wide, axes, 0, 0, tiled=True)


def row_shift(values, hops):
    size = lax.axis_size("img")
    pairs = [(i, i + hops) for i in range(size) if 0 <= i + hops < size]
    return lax.ppermute(values, "img", pairs)


def with_halo(values, width):
    rows = values.shape[0]
    before, after = [], []
    need, hop = width, 1
    while need > 0:
        part = min(need, rows)
        before.insert(0, row_shift(values[rows - part :], hop))
        after.append(row_shift(values[:part], -hop))
        need -= part
        hop += 1
    return jnp.concatenate(before + [values] + after, axis=0)


def planes_stack(field, width):
    rows = field.shape[0] - 2
    planes = jnp.pad(field.reshape(field.shape[0], 2, width), ((0, 0), (0, 0), (0, LANES - width)))
    stacked = jnp.concatenate([planes[i : i + rows] for i in range(3)], axis=1)
    return jnp.pad(stacked, ((0, 0), (0, 2), (0, 0))).astype(bf16)


def adamw(weight, grad, first_m, second_m, rate, decay, step_value):
    mean_new = beta_one * first_m + (1.0 - beta_one) * grad
    square_new = beta_two * second_m + (1.0 - beta_two) * grad * grad
    mean_hat = mean_new / (1.0 - beta_one**step_value)
    square_hat = square_new / (1.0 - beta_two**step_value)
    updated = weight - rate * (mean_hat / (jnp.sqrt(square_hat) + adam_epsilon) + decay * weight)
    return (updated, mean_new, square_new)


def body(
    kspace_data, coil_maps, sample_mask, valid_mask, target,
    first_weight, middle_weights, last_weight, norm_params, penalty,
    first_mean, first_square, middle_mean, middle_square, last_mean, last_square,
    norm_mean, norm_square, penalty_mean, penalty_square, step_count,
):
    n_img = lax.axis_size("img")
    n_ch = lax.axis_size("ch")
    n_all = n_img * n_ch
    own_ch = lax.axis_index("ch")
    own_img = lax.axis_index("img")
    coils = kspace_data.shape[1]
    height = kspace_data.shape[3]
    width = coil_maps.shape[4]
    rows = coil_maps.shape[3]
    cols = kspace_data.shape[4]
    wide = 2 * width
    per_dev = -(-coils // n_img)
    right_forward, right_back, left = dft_tables(width)

    lanes = rup(coils * cols, 128)
    (spec,) = call(
        spec_rows_kernel, [((height, 2 * lanes), bf16)], kspace_data[0], sample_mask[0], left,
        scratch=[pltpu.VMEM((height, 2 * lanes), f32)], name="spec_rows",
    )
    spec = lax.all_to_all(spec.reshape(n_img, rows, 2 * lanes), "img", 0, 0, tiled=True)
    (initial,) = call(
        initial_kernel, [((rows, wide), f32)], spec, coil_maps[0], right_back,
        scratch=[pltpu.VMEM((coils * rup(rows, 8), wide), f32), pltpu.VMEM((rows, wide), f32)], name="initial",
    )

    packed = jnp.concatenate(
        [middle_weights.reshape(-1), first_weight.reshape(-1), last_weight.reshape(-1), norm_params.reshape(-1)]
    )
    packed = jnp.pad(packed, (0, rup(packed.size, 1024) - packed.size)).reshape(-1, 128)
    everyone = spread(packed, "ch", n_ch).reshape(n_ch, -1)
    sizes = [middle_weights.size, first_weight.size, last_weight.size, norm_params.size]
    cuts = np.cumsum([0] + sizes)
    shapes = [middle_weights.shape, first_weight.shape, last_weight.shape, norm_params.shape]
    channel_dim = [2, 1, 2, 2]

    def full(k):
        piece = everyone[:, cuts[k] : cuts[k + 1]].reshape((n_ch,) + shapes[k])
        piece = jnp.moveaxis(piece, 0, channel_dim[k])
        dims = list(shapes[k])
        dims[channel_dim[k]] *= n_ch
        return piece.reshape(dims)

    middle_all, first_all, last_all, norms_all = (full(k) for k in range(4))
    low = middle_all.astype(bf16).reshape(3, 3, 3, CH, CH)
    forward_w = low.transpose(0, 2, 3, 1, 4).reshape(3, 3 * CH, 3 * CH)
    back_w = low[:, ::-1, ::-1].transpose(0, 2, 4, 1, 3).reshape(3, 3 * CH, 3 * CH)
    first_low = first_all.astype(bf16).reshape(3, 3, CH, 2)
    first_w = jnp.pad(first_low.transpose(1, 2, 0, 3).reshape(3 * CH, 6), ((0, 0), (0, 2)))
    last_low = last_all.astype(bf16).reshape(3, 3, 2, CH)
    last_w = jnp.pad(last_low.transpose(1, 2, 0, 3), ((0, 0), (0, 6), (0, 0), (0, 0))).reshape(24, 3 * CH)
    last_back_w = jnp.pad(last_low[::-1, ::-1].transpose(1, 3, 0, 2).reshape(3 * CH, 6), ((0, 0), (0, 2)))
    gain_bias = norms_all.reshape(4, 1, 2 * CH)

    maps_cat = jnp.concatenate([coil_maps[0, :, 0], coil_maps[0, :, 1]], axis=-1).astype(bf16)
    maps_cat = jnp.pad(maps_cat, ((0, per_dev * n_img - coils), (0, 0), (0, 0))).reshape(n_img, per_dev * rows, wide)
    target_cat = jnp.concatenate([target[0, 0], target[0, 1]], axis=-1).astype(bf16)
    valid_own = lax.dynamic_index_in_dim(valid_mask, own_ch, 0, keepdims=False)
    flags = jnp.concatenate([valid_own, sample_mask[0].T], axis=-1).astype(bf16)
    common = jnp.broadcast_to(jnp.concatenate([target_cat, flags], axis=0)[None], (n_img, 2 * rows, wide))
    early = lax.all_to_all(jnp.concatenate([maps_cat, common], axis=1), "img", 0, 0, tiled=True)
    early = early.reshape(n_img, per_dev + 2, rows, wide)
    maps_full = early[:, :per_dev].transpose(1, 0, 2, 3).reshape(per_dev, height, wide)
    target_full = early[:, per_dev].reshape(height, wide).astype(f32)
    flags = early[:, per_dev + 1].reshape(height, wide).astype(f32)
    valid2 = jnp.concatenate([flags[:, :width]] * 2, axis=1)
    mask2 = jnp.concatenate([flags[:, width:].T] * 2, axis=1)

    row_at = own_img * rows - HALO + jnp.arange(rows + 2 * HALO)
    in_image = ((row_at >= 0) & (row_at < height)).astype(f32)
    in_lane = (jnp.arange(LANES) < width).astype(f32)
    inside = in_image[:, None] * in_lane[None, :]
    is_own = ((row_at >= own_img * rows) & (row_at < (own_img + 1) * rows)).astype(f32)
    valid_pad = jnp.pad(valid_own.astype(bf16), ((0, 0), (0, LANES - width)))
    valid_rows = with_halo(valid_pad, 3).astype(f32)
    valid_rows = jnp.pad(valid_rows, ((HALO - 3, HALO - 3), (0, 0)))
    own_valid = valid_rows * is_own[:, None]
    own_lane = is_own[:, None] * in_lane[None, :]
    local_count = jnp.sum(valid_own.astype(f32))[None]
    vm = pl.BlockSpec(memory_space=pltpu.VMEM)
    sm = pl.BlockSpec(memory_space=pltpu.SMEM)

    def part(values, width_):
        return values[HALO - width_ : HALO + rows + width_]

    def exchange(values):
        return lax.all_to_all(values, BOTH, 0, 0, tiled=True)

    sums_shape = ((2 * n_all, 128), f32)

    stacked = planes_stack(with_halo(initial, HALO), width)
    hidden1, sums = pl.pallas_call(
        first_conv_kernel,
        out_shape=[jax.ShapeDtypeStruct((rows + 12, CH, LANES), f32), jax.ShapeDtypeStruct(*sums_shape)],
        in_specs=[vm, vm, vm, sm],
        compiler_params=params(), name="conv1",
    )(stacked, first_w, part(own_valid, 6), local_count)
    stats = [exchange(sums)]
    hidden = [hidden1]
    acts = []
    for layer in range(3):
        reach = 6 - layer
        act, out, sums = pl.pallas_call(
            conv_kernel,
            out_shape=[
                jax.ShapeDtypeStruct((rows + 2 * reach, CH, LANES), bf16),
                jax.ShapeDtypeStruct((rows + 2 * reach - 2, CH, LANES), f32),
                jax.ShapeDtypeStruct(*sums_shape),
            ],
            in_specs=[vm] * 6 + [sm], compiler_params=params(), name=f"conv{layer + 2}",
        )(
            hidden[layer], stats[layer], gain_bias[layer], forward_w[layer],
            part(inside, reach), part(own_valid, reach - 1), local_count,
        )
        acts.append(act)
        hidden.append(out)
        stats.append(exchange(sums))
    act4, branch = call(
        lambda *refs: last_conv_kernel(*refs, skip=2),
        [((rows + 2, CH, LANES), bf16), ((rows, 8, LANES), f32)],
        hidden[3], stats[3], gain_bias[3], last_w, part(inside, 3), name="conv5",
    )
    denoised = initial + branch[:, :2, :width].reshape(rows, wide)
    penalty_value = penalty[0]
    right_own = (initial + penalty_value * denoised).astype(bf16)

    right = spread(right_own, "img", n_img)
    tables = (right_forward, right_back, left)

    def reduced(partial):
        got = lax.all_to_all(partial, "img", 0, 0, tiled=True)
        return jnp.sum(got.reshape(n_img, rows, wide).astype(f32), axis=0).astype(bf16)

    (partial,) = call(
        solve_first_kernel, [((height, wide), bf16)],
        right, maps_full, mask2, *tables, name="solve1",
    )
    applied0 = spread(reduced(partial), "img", n_img)
    (partial,) = pl.pallas_call(
        solve_second_kernel,
        out_shape=[jax.ShapeDtypeStruct((height, wide), bf16)],
        in_specs=[vm, vm, vm, vm, sm, vm, vm, vm], compiler_params=params(), name="solve2",
    )(right, applied0, maps_full, mask2, penalty, *tables)
    applied1 = spread(reduced(partial), "img", n_img)
    count = jnp.sum(stats[0][1::2, 0])[None]
    partial, rest, scalars = pl.pallas_call(
        solve_back_kernel,
        out_shape=[
            jax.ShapeDtypeStruct((height, wide), bf16),
            jax.ShapeDtypeStruct((height, wide), f32),
            jax.ShapeDtypeStruct((8, 128), f32),
        ],
        in_specs=[vm] * 7 + [sm, sm] + [vm] * 3, compiler_params=params(), name="solve3",
    )(right, applied0, applied1, maps_full, mask2, target_full, valid2, penalty, count, *tables)
    reach = 4
    tall = jnp.pad(partial, ((reach, reach), (0, 0)))
    windows = jnp.concatenate([tall[rows * d : rows * d + rows + 2 * reach] for d in range(n_img)], axis=0)
    windows = lax.all_to_all(windows, "img", 0, 0, tiled=True).reshape(n_img, rows + 2 * reach, wide)
    rest_own = lax.dynamic_slice_in_dim(jnp.pad(rest, ((reach, reach), (0, 0))), own_img * rows, rows + 2 * reach, 0)
    grad_right = rest_own + jnp.sum(windows.astype(f32), axis=0)
    pen_part = scalars[0, 1] / n_img + jnp.sum(grad_right[reach : reach + rows] * denoised)
    loss_part = scalars[0, 0] / n_img
    grad_den = penalty_value * grad_right

    grad_stack = planes_stack(grad_den, width)
    gy, sums = call(
        back_last_kernel, [((rows + 6, CH, LANES), f32), sums_shape],
        grad_stack, last_back_w, hidden[3], stats[3], gain_bias[3], part(inside, 3), part(own_lane, 3), name="back5",
    )
    back_stats = [None] * 4
    back_stats[3] = exchange(sums)
    own_grad = jnp.pad(
        grad_den[reach : reach + rows].reshape(rows, 2, width), ((0, 0), (0, 6), (0, LANES - width))
    ).astype(bf16)
    (grad_last,) = call(
        lambda *refs: weight_grad_kernel(*refs, rows=rows, grad_skip=0, act_skip=0, stacked=False),
        [((24, 3 * CH), f32)], own_grad, act4, name="wgrad5",
    )
    grad_middle = [None] * 3
    for layer in (3, 2, 1):
        reach = layer
        grad, gy_next, sums = call(
            lambda *refs: back_kernel(*refs, skip_in=6 - 2 * layer, skip=8 - 2 * layer),
            [((rows + 2 * reach, CH, LANES), bf16), ((rows + 2 * reach - 2, CH, LANES), f32), sums_shape],
            gy, hidden[layer], stats[layer], back_stats[layer], gain_bias[layer],
            part(valid_rows, reach), back_w[layer - 1],
            hidden[layer - 1], stats[layer - 1], gain_bias[layer - 1],
            part(inside, 7 - layer), part(own_lane, reach - 1), name=f"back{layer + 1}",
        )
        gy = gy_next
        back_stats[layer - 1] = exchange(sums)
        (grad_middle[layer - 1],) = call(
            lambda *refs: weight_grad_kernel(*refs, rows=rows, grad_skip=reach, act_skip=6 - layer, stacked=False),
            [((3 * CH, 3 * CH), f32)], grad, acts[layer - 1], name=f"wgrad{layer + 1}",
        )
    (grad_first,) = call(
        lambda *refs: first_back_kernel(*refs, hidden_skip=6, stack_skip=6),
        [((3 * CH, 8), f32)], gy, hidden[0], stats[0], back_stats[0], gain_bias[0],
        part(valid_rows, 0), stacked, name="back1",
    )

    middle = jnp.stack(grad_middle).reshape(3, 3, CH, 3 * CH)
    share = 3 * 3 * (CH // n_ch) * 3 * CH // n_img
    lane = 128 if share % 128 == 0 else share
    blocks = middle.transpose(2, 0, 1, 3).reshape(n_all * share // lane, lane)
    got = lax.all_to_all(blocks, ("ch", "img"), 0, 0, tiled=True)
    mine = jnp.sum(got.reshape(n_all, share // lane, lane), axis=0)
    mine = spread(mine, "img", n_img)
    middle_own = mine.reshape(CH // n_ch, 3, 3, 3, CH)
    grad_middle_own = middle_own.transpose(1, 3, 2, 0, 4).reshape(middle_weights.shape)

    norm_sums = jnp.stack([jnp.sum(s[::2], axis=0) for s in back_stats])
    small = jnp.concatenate(
        [grad_first.reshape(-1), grad_last.reshape(3, 8, 3 * CH)[:, :2].reshape(-1), loss_part[None], pen_part[None]]
    )
    small = jnp.pad(small, (0, rup(small.size, 1024) - small.size)).reshape(-1, 128)
    total = jnp.sum(spread(small, BOTH, n_all).reshape(n_all, -1), axis=0)
    n_first = 3 * CH * 8
    first_full = total[:n_first].reshape(3, CH, 8)[:, :, :6].reshape(3, CH, 3, 2)
    first_full = first_full.transpose(2, 0, 1, 3).reshape(9, CH, 2)
    n_last = 3 * 2 * 3 * CH
    last_full = total[n_first : n_first + n_last].reshape(3, 2, 3, CH).transpose(2, 0, 1, 3).reshape(9, 2, CH)
    loss_value = total[n_first + n_last]
    grad_penalty = total[n_first + n_last + 1]
    own = CH // n_ch
    grad_first_own = lax.dynamic_slice_in_dim(first_full, own_ch * own, own, 1)
    grad_last_own = lax.dynamic_slice_in_dim(last_full, own_ch * own, own, 2)
    norm_full = norm_sums.reshape(4, 2, CH)[:, ::-1]
    grad_norm_own = lax.dynamic_slice_in_dim(norm_full, own_ch * own, own, 2)

    step_value = step_count[0].astype(f32) + 1.0
    first_out = adamw(first_weight, grad_first_own, first_mean, first_square, rate_conv, decay_rate, step_value)
    middle_out = adamw(middle_weights, grad_middle_own, middle_mean, middle_square, rate_conv, decay_rate, step_value)
    last_out = adamw(last_weight, grad_last_own, last_mean, last_square, rate_conv, decay_rate, step_value)
    norm_out = adamw(norm_params, grad_norm_own, norm_mean, norm_square, rate_norm, 0.0, step_value)
    penalty_out = adamw(penalty, grad_penalty[None], penalty_mean, penalty_square, rate_penalty, 0.0, step_value)
    return (loss_value,) + first_out + middle_out + last_out + norm_out + (jnp.concatenate(penalty_out),)


def solution(mesh):
    in_specs = (
        P("ch", None, None, None, "img"),
        P("ch", None, None, "img", None),
        P("ch", None, "img"),
        P(None, "img", None),
        P("ch", None, "img", None),
        P(None, "ch", None),
        P(None, None, "ch", None),
        P(None, None, "ch"),
        P(None, None, "ch"),
        P(),
        P(None, "ch", None),
        P(None, "ch", None),
        P(None, None, "ch", None),
        P(None, None, "ch", None),
        P(None, None, "ch"),
        P(None, None, "ch"),
        P(None, None, "ch"),
        P(None, None, "ch"),
        P(),
        P(),
        P(),
    )
    out_specs = (
        P(),
        P(None, "ch", None),
        P(None, "ch", None),
        P(None, "ch", None),
        P(None, None, "ch", None),
        P(None, None, "ch", None),
        P(None, None, "ch", None),
        P(None, None, "ch"),
        P(None, None, "ch"),
        P(None, None, "ch"),
        P(None, None, "ch"),
        P(None, None, "ch"),
        P(None, None, "ch"),
        P(),
    )
    return jax.shard_map(body, mesh=mesh, in_specs=in_specs, out_specs=out_specs, check_vma=False)
```

time: 2250 us -> 553 us (0.25)
  matrix products: 882 us -> 0 us
  blocking collectives: 464 us -> 47 us
  local copies, waits for them, and re-layouts: 406 us -> 72.1 us
  Pallas kernels: 0 us -> 209 us
  waiting for transfers between devices: 269 us -> 115 us
  other arithmetic: 110 us -> 16.8 us
  between operations: 46.4 us -> 8.7 us
    dot_general x198 -> x0, matrix products: 882 us -> none  [the longest x36 347 us: conv_input_grad(): jnp.einsum('oc,onhw->cnhw', weight[3 * row_shift + col_shift], window, pr...]
    psum x16 -> x0, blocking collectives: 353 us -> none  [the longest x6 120 us: image_sums(): return lax.psum(stacked, 'img')]
    pallas_call x0 -> x19, Pallas kernels: none -> 209 us  [the longest x13 132 us: call(): pl.pallas_call(kernel, out_shape=[jax.ShapeDtypeStruct(s, d) for s, d in...]
    all_gather x3 -> x0, waiting for transfers between devices: 165 us -> none  [channels_full(): return lax.all_gather(values, 'ch', axis=0, tiled=True)]
    slice x16 -> x51, local copies, waits for them, and re-layouts: 170 us -> 18.3 us  [the longest x15 9.51 us: part(): return values[HALO - width_:HALO + rows + width_]]
    unnamed x356 -> x102, local copies, waits for them, and re-layouts: 121 us -> 22.7 us
    all_to_all x19 -> x1, local copies, waits for them, and re-layouts: 73.7 us -> 1.29 us  [body(): got = lax.all_to_all(blocks, ('ch', 'img'), 0, 0, tiled=True)]
    all_to_all x5 -> x3, blocking collectives: 99.8 us -> 47 us  [the longest x2 31.6 us: reduced(): got = lax.all_to_all(partial, 'img', 0, 0, tiled=True)]
  transfers between devices with their start and end apart: 30 -> 21, of which waited for: 16 -> 15; matrix products, arithmetic and copies ran while one was open for 18% -> 10% of each run, Pallas kernels for 0% -> 9%
where the time goes in v1:
time: 553 us; the launch traced here: 542 us
  Pallas kernels  209 us (38%)
  waiting for transfers between devices  115 us (21%)
  starting transfers between devices  73.6 us (13%)
  local copies, waits for them, and re-layouts  72.1 us (13%)
  blocking collectives  47 us (8%)
  other arithmetic  16.8 us (3%)
  between operations  8.7 us (2%)
    pallas_call x13, Pallas kernels, call(): pl.pallas_call(kernel, out_shape=[jax.ShapeDtypeStruct(s, d) for s, d in...  132 us
    pallas_call x3, Pallas kernels, body(): pl.pallas_call(conv_kernel, out_shape=[jax.ShapeDtypeStruct((rows + 2 * r...  44.1 us
    all_to_all x8, waiting for transfers between devices, exchange(): return lax.all_to_all(values, BOTH, 0, 0, tiled=True)  34.3 us
    all_to_all x2, blocking collectives, reduced(): got = lax.all_to_all(partial, 'img', 0, 0, tiled=True)  31.6 us
    all_to_all x8, starting transfers between devices, exchange(): return lax.all_to_all(values, BOTH, 0, 0, tiled=True)  25.9 us
    all_to_all x1, waiting for transfers between devices, body(): lax.all_to_all(jnp.concatenate([maps_cat, common], axis=1), 'img', 0, 0,...  25.1 us
    all_to_all x5, waiting for transfers between devices, spread(): return lax.all_to_all(wide, axes, 0, 0, tiled=True)  23.2 us
    unnamed x102, local copies, waits for them, and re-layouts  22.7 us
  transfers between devices with their start and end apart: 21, of which 15 were waited for; matrix products, arithmetic and copies ran while one was open for 10% of the time, Pallas kernels for 9%

profile of v1, /device:TPU:0, one launch (start us, length us, event | category | flops | bytes accessed | tf_op | source)
XLA Modules:
  0.0 542.0 jit_solution(5264660201016107132)
XLA Ops:
  39.8 10.3 %all-to-all-done.spec = bf16[8,40,1024]{2,1,0:T(8,128)(2,1)S(1)} async-done(((bf16[8,40,1024]{2,1,0:T(8,128)(2,1)}), bf16[8,40,1024]{2,1,0:T(8,128)(2,1)S(1)}, u32[]{:S(2)}, u32[]{:S(2)}) %all-to-all-start) | async-done | bytes 655392 | tf_op jit(solution)/shard_map/all_to_all | solution.py:477
  68.1 12.1 %conv1.1 = (f32[52,64,384]{2,1,0:T(8,128)}, f32[64,128]{1,0:T(8,128)}) custom-call(bf16[52,8,384]{2,1,0:T(8,128)(2,1)} %fusion.10.stacked.refs_6_, bf16[192,8]{1,0:T(8,128)(2,1)} %pad.65.weight, f32[52,384]{1,0:T(8,128)} %slice.346.mask, f32[1]{0:T(128)} %bitcast.10.count), custom_call_target="tpu_custom_call" | custom-call | tf_op jit(solution)/shard_map/conv1/pallas_call | solution.py:548
  91.6 15.3 %conv2.1 = (bf16[52,64,384]{2,1,0:T(8,128)(2,1)}, f32[50,64,384]{2,1,0:T(8,128)}, f32[64,128]{1,0:T(8,128)}) custom-call(f32[52,64,384]{2,1,0:T(8,128)} %get-tuple-element.41.hidden.refs_7_.refs_1_, f32[64,128]{1,0:T(8,128)} %bitcast.144, f32[1,128]{1,0:T(1,128)} %squeeze.83.gain_bias.refs_9_.refs_4_, bf16[192,192]{1,0:T(8,128)(2,1)} %squeeze.84.weight, ...), custom_call_target="tpu_custom_call" | custom-call | tf_op jit(solution)/shard_map/conv2/pallas_call | solution.py:559
  117.2 14.7 %conv3.1 = (bf16[50,64,384]{2,1,0:T(8,128)(2,1)}, f32[48,64,384]{2,1,0:T(8,128)}, f32[64,128]{1,0:T(8,128)}) custom-call(f32[50,64,384]{2,1,0:T(8,128)} %get-tuple-element.43.hidden.refs_7_.refs_1_, f32[64,128]{1,0:T(8,128)} %bitcast.148, f32[1,128]{1,0:T(1,128)} %squeeze.85.gain_bias.refs_9_.refs_4_, bf16[192,192]{1,0:T(8,128)(2,1)} %squeeze.86.weight, ...), custom_call_target="tpu_custom_call" | custom-call | tf_op jit(solution)/shard_map/conv3/pallas_call | solution.py:559
  142.3 14.1 %conv4.1 = (bf16[48,64,384]{2,1,0:T(8,128)(2,1)}, f32[46,64,384]{2,1,0:T(8,128)}, f32[64,128]{1,0:T(8,128)}) custom-call(f32[48,64,384]{2,1,0:T(8,128)} %get-tuple-element.45.hidden.refs_7_.refs_1_, f32[64,128]{1,0:T(8,128)} %bitcast.151, f32[1,128]{1,0:T(1,128)} %squeeze.87.gain_bias.refs_9_.refs_4_, bf16[192,192]{1,0:T(8,128)(2,1)} %squeeze.88.weight, ...), custom_call_target="tpu_custom_call" | custom-call | tf_op jit(solution)/shard_map/conv4/pallas_call | solution.py:559
  172.8 9.1 %conv5.1 = (bf16[42,64,384]{2,1,0:T(8,128)(2,1)}, f32[40,8,384]{2,1,0:T(8,128)}) custom-call(f32[46,64,384]{2,1,0:T(8,128)} %get-tuple-element.47.refs_0_.hidden.refs_1_, f32[64,128]{1,0:T(8,128)} %bitcast.154, f32[1,128]{1,0:T(1,128)} %squeeze.89.refs_2_.gain_bias.refs_4_, bf16[24,192]{1,0:T(8,128)(2,1)} %reshape.294.refs_3_, f32[46,384]{1,0:T(8,128)} %slice.363.refs_4_.inside), custom_call_target="tpu_custom_call" | custom-call | tf_op jit(solution)/shard_map/conv5/pallas_call | solution.py:37
  183.7 25.1 %all-to-all-done.7 = bf16[8,160,640]{2,1,0:T(8,128)(2,1)S(1)} async-done(((bf16[8,160,640]{2,1,0:T(8,128)(2,1)}), bf16[8,160,640]{2,1,0:T(8,128)(2,1)S(1)}, u32[]{:S(2)}, u32[]{:S(2)}) %all-to-all-start.7) | async-done | bytes 1638432 | tf_op jit(solution)/shard_map/all_to_all | solution.py:517
  217.4 8.0 %all-to-all-done.6 = bf16[8,40,640]{2,1,0:T(8,128)(2,1)S(1)} async-done(((bf16[8,40,640]{2,1,0:T(8,128)(2,1)}), bf16[8,40,640]{2,1,0:T(8,128)(2,1)S(1)}, u32[]{:S(2)}, u32[]{:S(2)}) %all-to-all-start.6) | async-done | bytes 409632 | tf_op jit(solution)/shard_map/all_to_all | solution.py:414
  233.9 16.1 %all_to_all.176 = bf16[8,40,640]{2,1,0:T(8,128)(2,1)S(1)} all-to-all(bf16[8,40,640]{2,1,0:T(8,128)(2,1)} %bitcast.134), channel_id=1, replica_groups=mesh['img'=8,'ch'=4] {'img'}, dimensions={0} | all-to-all | bytes 819200 | tf_op jit(solution)/shard_map/all_to_all | solution.py:587
  250.1 15.4 %all_to_all.177 = bf16[8,40,640]{2,1,0:T(8,128)(2,1)} all-to-all(bf16[8,40,640]{2,1,0:T(8,128)(2,1)S(1)} %broadcast_in_dim.31), channel_id=1, replica_groups=mesh['img'=8,'ch'=4] {'img'}, dimensions={0} | all-to-all | bytes 819200 | tf_op jit(solution)/shard_map/all_to_all | solution.py:414
  265.5 8.6 %solve2.1 = bf16[320,640]{1,0:T(8,128)(2,1)} custom-call(bf16[320,640]{1,0:T(8,128)(2,1)} %bitcast.122, bf16[320,640]{1,0:T(8,128)(2,1)} %bitcast.129, bf16[2,320,640]{2,1,0:T(8,128)(2,1)} %bitcast.117, f32[320,640]{1,0:T(8,128)} %copy.130.mask2, f32[1]{0:T(128)} %copy.160.penalty, bf16[640,640]{1,0:T(8,128)(2,1)} %constant.149.right_forward, ...), custom_call_target="tpu_custom_call" | custom-call | tf_op jit(solution)/shard_map/solve2/pallas_call | solution.py:595
  274.1 15.5 %all_to_all.178 = bf16[8,40,640]{2,1,0:T(8,128)(2,1)S(1)} all-to-all(bf16[8,40,640]{2,1,0:T(8,128)(2,1)} %bitcast.135), channel_id=1, replica_groups=mesh['img'=8,'ch'=4] {'img'}, dimensions={0} | all-to-all | bytes 819200 | tf_op jit(solution)/shard_map/all_to_all | solution.py:587
  296.9 8.6 %all-to-all-done.11 = bf16[8,40,640]{2,1,0:T(8,128)(2,1)S(1)} async-done(((bf16[8,40,640]{2,1,0:T(8,128)(2,1)}), bf16[8,40,640]{2,1,0:T(8,128)(2,1)S(1)}, u32[]{:S(2)}, u32[]{:S(2)}) %all-to-all-start.11) | async-done | bytes 409632 | tf_op jit(solution)/shard_map/all_to_all | solution.py:414
  306.3 11.9 %solve3.1 = (bf16[320,640]{1,0:T(8,128)(2,1)}, f32[320,640]{1,0:T(8,128)}, f32[8,128]{1,0:T(8,128)}) custom-call(bf16[320,640]{1,0:T(8,128)(2,1)} %bitcast.123, bf16[320,640]{1,0:T(8,128)(2,1)} %bitcast.130, bf16[320,640]{1,0:T(8,128)(2,1)} %bitcast.136, bf16[2,320,640]{2,1,0:T(8,128)(2,1)} %bitcast.118, f32[320,640]{1,0:T(8,128)} %copy.130.mask2, ...), custom_call_target="tpu_custom_call" | custom-call | tf_op jit(solution)/shard_map/solve3/pallas_call | solution.py:602
  336.2 11.0 %all-to-all-done.12 = bf16[8,48,640]{2,1,0:T(8,128)(2,1)S(1)} async-done(((bf16[8,48,640]{2,1,0:T(8,128)(2,1)}), bf16[8,48,640]{2,1,0:T(8,128)(2,1)S(1)}, u32[]{:S(2)}, u32[]{:S(2)}) %all-to-all-start.12) | async-done | bytes 491552 | tf_op jit(solution)/shard_map/all_to_all | solution.py:614
  348.7 12.3 %back5.1 = (f32[46,64,384]{2,1,0:T(8,128)}, f32[64,128]{1,0:T(8,128)}) custom-call(bf16[46,8,384]{2,1,0:T(8,128)(2,1)} %fusion.12.stacked, bf16[192,8]{1,0:T(8,128)(2,1)} %pad.74.weight, f32[46,64,384]{2,1,0:T(8,128)} %get-tuple-element.47.refs_0_.hidden.refs_1_, f32[64,128]{1,0:T(8,128)} %bitcast.155, f32[1,128]{1,0:T(1,128)} %squeeze.89.refs_2_.gain_bias.refs_4_, ...), custom_call_target="tpu_custom_call" | custom-call | tf_op jit(solution)/shard_map/back5/pallas_call | solution.py:37
  371.6 16.6 %back4.1 = (bf16[46,64,384]{2,1,0:T(8,128)(2,1)}, f32[44,64,384]{2,1,0:T(8,128)}, f32[64,128]{1,0:T(8,128)}) custom-call(f32[46,64,384]{2,1,0:T(8,128)} %get-tuple-element.52.refs_0_, f32[46,64,384]{2,1,0:T(8,128)} %get-tuple-element.47.refs_0_.hidden.refs_1_, f32[64,128]{1,0:T(8,128)} %bitcast.156, f32[64,128]{1,0:T(8,128)} %bitcast.161, ...), custom_call_target="tpu_custom_call" | custom-call | tf_op jit(solution)/shard_map/back4/pallas_call | solution.py:37
  398.6 16.1 %back3.1 = (bf16[44,64,384]{2,1,0:T(8,128)(2,1)}, f32[42,64,384]{2,1,0:T(8,128)}, f32[64,128]{1,0:T(8,128)}) custom-call(f32[44,64,384]{2,1,0:T(8,128)} %get-tuple-element.54.refs_0_, f32[48,64,384]{2,1,0:T(8,128)} %get-tuple-element.45.hidden.refs_7_.refs_1_, f32[64,128]{1,0:T(8,128)} %bitcast.153, f32[64,128]{1,0:T(8,128)} %bitcast.163, ...), custom_call_target="tpu_custom_call" | custom-call | tf_op jit(solution)/shard_map/back3/pallas_call | solution.py:37
  430.8 15.8 %back2.1 = (bf16[42,64,384]{2,1,0:T(8,128)(2,1)}, f32[40,64,384]{2,1,0:T(8,128)}, f32[64,128]{1,0:T(8,128)}) custom-call(f32[42,64,384]{2,1,0:T(8,128)} %get-tuple-element.56.refs_0_, f32[50,64,384]{2,1,0:T(8,128)} %get-tuple-element.43.hidden.refs_7_.refs_1_, f32[64,128]{1,0:T(8,128)} %bitcast.150, f32[64,128]{1,0:T(8,128)} %bitcast.165, ...), custom_call_target="tpu_custom_call" | custom-call | tf_op jit(solution)/shard_map/back2/pallas_call | solution.py:37
  460.3 10.4 %back1.1 = f32[192,8]{1,0:T(8,128)} custom-call(f32[40,64,384]{2,1,0:T(8,128)} %get-tuple-element.58.refs_0_, f32[52,64,384]{2,1,0:T(8,128)} %get-tuple-element.41.hidden.refs_7_.refs_1_, f32[64,128]{1,0:T(8,128)} %bitcast.146, f32[64,128]{1,0:T(8,128)} %bitcast.167, f32[1,128]{1,0:T(1,128)} %squeeze.83.gain_bias.refs_9_.refs_4_, f32[40,384]{1,0:T(8,128)} %slice.385.refs_5_, ...), custom_call_target="tpu_custom_call" | custom-call | tf_op jit(solution)/shard_map/back1/pallas_call | solution.py:37
  475.2 8.9 %wgrad4.1 = f32[192,192]{1,0:T(8,128)} custom-call(bf16[46,64,384]{2,1,0:T(8,128)(2,1)} %get-tuple-element.66.refs_0_, bf16[48,64,384]{2,1,0:T(8,128)(2,1)} %get-tuple-element.67.refs_1_), custom_call_target="tpu_custom_call" | custom-call | tf_op jit(solution)/shard_map/wgrad4/pallas_call | solution.py:37
  485.2 8.9 %wgrad3.1 = f32[192,192]{1,0:T(8,128)} custom-call(bf16[44,64,384]{2,1,0:T(8,128)(2,1)} %get-tuple-element.64.refs_0_, bf16[50,64,384]{2,1,0:T(8,128)(2,1)} %get-tuple-element.65.refs_1_), custom_call_target="tpu_custom_call" | custom-call | tf_op jit(solution)/shard_map/wgrad3/pallas_call | solution.py:37
  495.2 8.9 %wgrad2.1 = f32[192,192]{1,0:T(8,128)} custom-call(bf16[42,64,384]{2,1,0:T(8,128)(2,1)} %get-tuple-element.62.refs_0_, bf16[52,64,384]{2,1,0:T(8,128)(2,1)} %get-tuple-element.63.refs_1_), custom_call_target="tpu_custom_call" | custom-call | tf_op jit(solution)/shard_map/wgrad2/pallas_call | solution.py:37
  520.3 8.7 %all-to-all-done.18 = f32[32,27,128]{2,1,0:T(8,128)S(1)} async-done(((f32[32,27,128]{2,1,0:T(8,128)}), f32[32,27,128]{2,1,0:T(8,128)S(1)}, u32[]{:S(2)}, u32[]{:S(2)}) %all-to-all-start.18) | async-done | bytes 442400 | tf_op jit(solution)/shard_map/all_to_all | solution.py:662
  (310 shorter events, 230.7 us)
Async XLA Ops:
  5.1 20.7 %all-to-all-start.1 = ((f32[4,224,128]{2,1,0:T(8,128)}), f32[4,224,128]{2,1,0:T(8,128)S(1)}, u32[]{:S(2)}, u32[]{:S(2)}) async-start(f32[4,224,128]{2,1,0:T(8,128)} %broadcast_in_dim.27), calls=%async_computation.1 | async-start | bytes 917504 | tf_op jit(solution)/shard_map/all_to_all | solution.py:414
  10.2 25.5 %collective-permute-start.2 = (bf16[3,384]{1,0:T(4,128)(2,1)S(1)}, bf16[3,384]{1,0:T(4,128)(2,1)S(1)}, u32[]{:S(2)}, u32[]{:S(2)}) collective-permute-start(bf16[3,384]{1,0:T(4,128)(2,1)S(1)} %get-tuple-element.108), channel_id=1, source_target_pairs={{0,4},{4,8},{8,12},{12,16},{16,20},{20,24},{24,28},{1,5},{5,9},{9,... | collective-permute-start | bytes 6920 | tf_op jit(solution)/shard_map/ppermute | solution.py:420
  14.3 21.3 %collective-permute-start.3 = (bf16[3,384]{1,0:T(4,128)(2,1)S(1)}, bf16[3,384]{1,0:T(4,128)(2,1)S(1)}, u32[]{:S(2)}, u32[]{:S(2)}) collective-permute-start(bf16[3,384]{1,0:T(4,128)(2,1)S(1)} %get-tuple-element.109), channel_id=1, source_target_pairs={{4,0},{8,4},{12,8},{16,12},{20,16},{24,20},{28,24},{5,1},{9,5},{13... | collective-permute-start | bytes 6920 | tf_op jit(solution)/shard_map/ppermute | solution.py:420
  25.8 24.3 %all-to-all-start = ((bf16[8,40,1024]{2,1,0:T(8,128)(2,1)}), bf16[8,40,1024]{2,1,0:T(8,128)(2,1)S(1)}, u32[]{:S(2)}, u32[]{:S(2)}) async-start(bf16[8,40,1024]{2,1,0:T(8,128)(2,1)} %bitcast.132), calls=%async_computation | async-start | bytes 1310720 | tf_op jit(solution)/shard_map/all_to_all | solution.py:477
  56.8 6.6 %collective-permute-start = (bf16[7,640]{1,0:T(8,128)(2,1)S(1)}, bf16[7,640]{1,0:T(8,128)(2,1)S(1)}, u32[]{:S(2)}, u32[]{:S(2)}) collective-permute-start(bf16[7,640]{1,0:T(8,128)(2,1)S(1)} %get-tuple-element.98), channel_id=1, source_target_pairs={{0,4},{4,8},{8,12},{12,16},{16,20},{20,24},{24,28},{1,5},{5,9},{9,... | collective-permute-start | bytes 26888 | tf_op jit(solution)/shard_map/ppermute | solution.py:420
  60.1 5.6 %collective-permute-start.1 = (bf16[7,640]{1,0:T(8,128)(2,1)S(1)}, bf16[7,640]{1,0:T(8,128)(2,1)S(1)}, u32[]{:S(2)}, u32[]{:S(2)}) collective-permute-start(bf16[7,640]{1,0:T(8,128)(2,1)S(1)} %get-tuple-element.99), channel_id=1, source_target_pairs={{4,0},{8,4},{12,8},{16,12},{20,16},{24,20},{28,24},{5,1},{9,5},{13... | collective-permute-start | bytes 26888 | tf_op jit(solution)/shard_map/ppermute | solution.py:420
  80.1 10.8 %all-to-all-start.2 = ((f32[32,2,128]{2,1,0:T(2,128)}), f32[32,2,128]{2,1,0:T(2,128)S(1)}, u32[]{:S(2)}, u32[]{:S(2)}) async-start(f32[32,2,128]{2,1,0:T(2,128)} %bitcast.183), calls=%async_computation.2 | async-start | bytes 65536 | tf_op jit(solution)/shard_map/all_to_all | solution.py:543
  106.8 9.8 %all-to-all-start.3 = ((f32[32,2,128]{2,1,0:T(2,128)}), f32[32,2,128]{2,1,0:T(2,128)S(1)}, u32[]{:S(2)}, u32[]{:S(2)}) async-start(f32[32,2,128]{2,1,0:T(2,128)} %bitcast.181), calls=%async_computation.3 | async-start | bytes 65536 | tf_op jit(solution)/shard_map/all_to_all | solution.py:543
  132.0 9.7 %all-to-all-start.4 = ((f32[32,2,128]{2,1,0:T(2,128)}), f32[32,2,128]{2,1,0:T(2,128)S(1)}, u32[]{:S(2)}, u32[]{:S(2)}) async-start(f32[32,2,128]{2,1,0:T(2,128)} %bitcast.180), calls=%async_computation.4 | async-start | bytes 65536 | tf_op jit(solution)/shard_map/all_to_all | solution.py:543
  156.4 9.7 %all-to-all-start.5 = ((f32[32,2,128]{2,1,0:T(2,128)}), f32[32,2,128]{2,1,0:T(2,128)S(1)}, u32[]{:S(2)}, u32[]{:S(2)}) async-start(f32[32,2,128]{2,1,0:T(2,128)} %bitcast.185), calls=%async_computation.5 | async-start | bytes 65536 | tf_op jit(solution)/shard_map/all_to_all | solution.py:543
  166.2 42.6 %all-to-all-start.7 = ((bf16[8,160,640]{2,1,0:T(8,128)(2,1)}), bf16[8,160,640]{2,1,0:T(8,128)(2,1)S(1)}, u32[]{:S(2)}, u32[]{:S(2)}) async-start(bf16[8,160,640]{2,1,0:T(8,128)(2,1)} %pad_maximum_fusion), calls=%async_computation.7 | async-start | bytes 3276800 | tf_op jit(solution)/shard_map/all_to_all | solution.py:517
  209.6 15.9 %all-to-all-start.6 = ((bf16[8,40,640]{2,1,0:T(8,128)(2,1)}), bf16[8,40,640]{2,1,0:T(8,128)(2,1)S(1)}, u32[]{:S(2)}, u32[]{:S(2)}) async-start(bf16[8,40,640]{2,1,0:T(8,128)(2,1)} %broadcast_in_dim.29), calls=%async_computation.6 | async-start | bytes 819200 | tf_op jit(solution)/shard_map/all_to_all | solution.py:414
  290.4 15.1 %all-to-all-start.11 = ((bf16[8,40,640]{2,1,0:T(8,128)(2,1)}), bf16[8,40,640]{2,1,0:T(8,128)(2,1)S(1)}, u32[]{:S(2)}, u32[]{:S(2)}) async-start(bf16[8,40,640]{2,1,0:T(8,128)(2,1)} %broadcast_in_dim.32), calls=%async_computation.11 | async-start | bytes 819200 | tf_op jit(solution)/shard_map/all_to_all | solution.py:414
  330.3 16.9 %all-to-all-start.12 = ((bf16[8,48,640]{2,1,0:T(8,128)(2,1)}), bf16[8,48,640]{2,1,0:T(8,128)(2,1)S(1)}, u32[]{:S(2)}, u32[]{:S(2)}) async-start(bf16[8,48,640]{2,1,0:T(8,128)(2,1)} %bitcast.45), calls=%async_computation.12 | async-start | bytes 983040 | tf_op jit(solution)/shard_map/all_to_all | solution.py:614
  361.0 10.0 %all-to-all-start.13 = ((f32[32,2,128]{2,1,0:T(2,128)}), f32[32,2,128]{2,1,0:T(2,128)S(1)}, u32[]{:S(2)}, u32[]{:S(2)}) async-start(f32[32,2,128]{2,1,0:T(2,128)} %bitcast.184), calls=%async_computation.13 | async-start | bytes 65536 | tf_op jit(solution)/shard_map/all_to_all | solution.py:543
  388.2 9.8 %all-to-all-start.14 = ((f32[32,2,128]{2,1,0:T(2,128)}), f32[32,2,128]{2,1,0:T(2,128)S(1)}, u32[]{:S(2)}, u32[]{:S(2)}) async-start(f32[32,2,128]{2,1,0:T(2,128)} %bitcast.179), calls=%async_computation.14 | async-start | bytes 65536 | tf_op jit(solution)/shard_map/all_to_all | solution.py:543
  414.7 15.5 %all-to-all-start.15 = ((f32[32,2,128]{2,1,0:T(2,128)}), f32[32,2,128]{2,1,0:T(2,128)S(1)}, u32[]{:S(2)}, u32[]{:S(2)}) async-start(f32[32,2,128]{2,1,0:T(2,128)} %bitcast.178), calls=%async_computation.15 | async-start | bytes 65536 | tf_op jit(solution)/shard_map/all_to_all | solution.py:543
  446.6 13.1 %all-to-all-start.16 = ((f32[32,2,128]{2,1,0:T(2,128)}), f32[32,2,128]{2,1,0:T(2,128)S(1)}, u32[]{:S(2)}, u32[]{:S(2)}) async-start(f32[32,2,128]{2,1,0:T(2,128)} %bitcast.182), calls=%async_computation.16 | async-start | bytes 65536 | tf_op jit(solution)/shard_map/all_to_all | solution.py:543
  472.6 34.3 %all-to-all-start.17 = ((f32[32,24,128]{2,1,0:T(8,128)}), f32[32,24,128]{2,1,0:T(8,128)S(1)}, u32[]{:S(2)}, u32[]{:S(2)}) async-start(f32[32,24,128]{2,1,0:T(8,128)} %broadcast_in_dim.72), calls=%async_computation.17 | async-start | bytes 786432 | tf_op jit(solution)/shard_map/all_to_all | solution.py:414
  506.8 33.8 %copy-start.11 = (f32[3,9,16,64]{3,2,1,0:T(8,128)S(1)}, f32[3,9,16,64]{3,2,1,0:T(8,128)}, u32[]{:S(2)}) copy-start(f32[3,9,16,64]{3,2,1,0:T(8,128)} %param.30) | copy-start | bytes 331780
  506.8 33.8 %copy-start.22 = (f32[3,9,16,64]{3,2,1,0:T(8,128)S(1)}, f32[3,9,16,64]{3,2,1,0:T(8,128)}, u32[]{:S(2)}) copy-start(f32[3,9,16,64]{3,2,1,0:T(8,128)} %param.37) | copy-start | bytes 331780
  506.8 33.8 %copy-start.23 = (f32[3,9,16,64]{3,2,1,0:T(8,128)S(1)}, f32[3,9,16,64]{3,2,1,0:T(8,128)}, u32[]{:S(2)}) copy-start(f32[3,9,16,64]{3,2,1,0:T(8,128)} %param.36) | copy-start | bytes 331780
  506.8 22.2 %all-to-all-start.18 = ((f32[32,27,128]{2,1,0:T(8,128)}), f32[32,27,128]{2,1,0:T(8,128)S(1)}, u32[]{:S(2)}, u32[]{:S(2)}) async-start(f32[32,27,128]{2,1,0:T(8,128)} %all_to_all.153), calls=%async_computation.18 | async-start | bytes 1048576 | tf_op jit(solution)/shard_map/all_to_all | solution.py:662
  529.8 10.7 %all-to-all-start.19 = ((f32[8,27,128]{2,1,0:T(8,128)}), f32[8,27,128]{2,1,0:T(8,128)S(1)}, u32[]{:S(2)}, u32[]{:S(2)}) async-start(f32[8,27,128]{2,1,0:T(8,128)} %broadcast_in_dim.73), calls=%async_computation.19 | async-start | bytes 262144 | tf_op jit(solution)/shard_map/all_to_all | solution.py:414
  (42 other events, 494.5 us)

commit v2 on v1

v2 whole, which is shorter than its diff:
```python
import math

import jax
import jax.numpy as jnp
import numpy as np
from jax import lax
from jax.experimental import pallas as pl
from jax.experimental.pallas import tpu as pltpu
from jax.sharding import PartitionSpec as P

norm_epsilon = 1e-05
beta_one = 0.9
beta_two = 0.999
adam_epsilon = 1e-08
decay_rate = 0.01
rate_conv = 0.04
rate_norm = 0.1
rate_penalty = 0.01

BOTH = ("img", "ch")
f32 = jnp.float32
bf16 = jnp.bfloat16
CH = 64
LANES = 384
HALO = 7


def rup(n, m):
    return (n + m - 1) // m * m


VM = pl.BlockSpec(memory_space=pltpu.VMEM)
SM = pl.BlockSpec(memory_space=pltpu.SMEM)
HB = pl.BlockSpec(memory_space=pltpu.HBM)


def call(kernel, ins, outs, args, scratch=(), name=None, mb=60):
    return pl.pallas_call(
        kernel,
        out_shape=[jax.ShapeDtypeStruct(shape, dtype) for shape, dtype, _ in outs],
        in_specs=ins,
        out_specs=[spec for _, _, spec in outs],
        scratch_shapes=list(scratch),
        compiler_params=pltpu.CompilerParams(vmem_limit_bytes=mb * 1024 * 1024),
        name=name,
    )(*args)


def dft_tables(n):
    k = np.arange(n)
    angle = (k[:, None] * k[None, :] % n) * (2.0 * math.pi / n)
    exact = np.concatenate([np.cos(angle), np.sin(angle)], 0) / math.sqrt(n)

    def rounded(factor):
        return (factor * exact).astype(np.float32).astype(bf16)

    def bias(factor):
        return abs(np.vdot(exact, rounded(factor).astype(np.float64) / factor) / np.vdot(exact, exact) - 1.0)

    factor = min((1.0 + 0.005 * step for step in range(201)), key=bias)
    left = lax.optimization_barrier(jnp.asarray(rounded(factor)))
    cosine, sine = left[:n], left[n:]
    right_forward = jnp.concatenate([left, jnp.concatenate([-sine, cosine], 0)], 1)
    right_back = jnp.concatenate(
        [jnp.concatenate([cosine, -sine], 0), jnp.concatenate([sine, cosine], 0)], 1
    )
    return right_forward, right_back, left, factor


def swap(values):
    return pltpu.roll(values, values.shape[-1] // 2, values.ndim - 1)


def first_half(shape):
    return lax.broadcasted_iota(jnp.int32, shape, len(shape) - 1) < shape[-1] // 2


def mm(a, b):
    return jnp.dot(a, b, preferred_element_type=f32)


def left_dft(left, values, inverse):
    rows = left.shape[0] // 2
    both = mm(left, values)
    plain, crossed = both[:rows], swap(both[rows:])
    half = first_half(plain.shape)
    crossed = jnp.where(half, crossed, -crossed)
    return plain - crossed if inverse else plain + crossed


def map_pair(cat):
    half = first_half(cat.shape)
    other = swap(cat)
    return jnp.where(half, cat, other), jnp.where(half, -other, cat)


def message_kernel(kspace, mask, maps, target, any_rows, any_cols, left, out, gathered, tall, *, at_maps):
    coils, _, cols, height = kspace.shape
    devices, length, wide = out.shape
    width = wide // 2
    rows = height // devices
    window = rows + 2 * HALO
    block = rup(window, 8)
    used = coils * cols
    half = rup(used, 128)
    pad = (tall.shape[0] - height) // 2
    gathered[...] = jnp.zeros(gathered.shape, f32)
    sampled = mask[...].astype(f32)
    for part in range(2):
        for coil in range(coils):
            at = part * half + coil * cols
            gathered[at : at + cols] = kspace[coil, part] * sampled
    tall[:pad] = jnp.zeros((pad, 2 * half), f32)
    tall[pad + height :] = jnp.zeros((pad, 2 * half), f32)
    both = outer(left[...], gathered[...].astype(bf16))
    crossed = swap(both[height:])
    crossed = jnp.where(first_half(crossed.shape), -crossed, crossed)
    tall[pad : pad + height] = both[:height] + crossed
    sampled = sampled.astype(bf16)
    per_dev = (length - at_maps) // rows - 1
    for d in range(devices):
        first = pad + d * rows - HALO
        view = tall[first : first + window].astype(bf16)
        for part in range(2):
            to = part * block
            out[d, to : to + window, :used] = view[:, part * half : part * half + used]
            out[d, to : to + cols, wide - width // 2 :] = sampled[:, part * (width // 2) : (part + 1) * (width // 2)]
        out[d, block + cols : block + cols + 2, wide - width // 2 :] = any_cols[...]
        out[d, block + cols + 2 : block + cols + 3, wide - width // 2 : wide - width // 2 + rows] = any_rows[...]
        for k in range(per_dev):
            to = at_maps + k * rows
            coil = d * per_dev + k
            if coil < coils:
                out[d, to : to + rows, :width] = maps[coil, 0].astype(bf16)
                out[d, to : to + rows, width:] = maps[coil, 1].astype(bf16)
            else:
                out[d, to : to + rows] = jnp.zeros((rows, wide), bf16)
        to = at_maps + per_dev * rows
        out[d, to : to + rows, :width] = target[0].astype(bf16)
        out[d, to : to + rows, width:] = target[1].astype(bf16)


def stack_rows(field, first, second, out):
    width = field.shape[1] // 2
    rows = out.shape[0]
    for plane_at, at in ((first, 0), (second, width)):
        plane_at[:, width:] = jnp.zeros((field.shape[0], LANES - width), f32)
        plane_at[:, :width] = field[:, at : at + width]
    out[...] = jnp.zeros(out.shape, f32)

    def move(r, carry):
        for i in range(3):
            out[r, 2 * i : 2 * i + 1, :] = first[pl.ds(r + i, 1), :]
            out[r, 2 * i + 1 : 2 * i + 2, :] = second[pl.ds(r + i, 1), :]
        return carry

    lax.fori_loop(0, rows, move, 0)


def initial_kernel(message, maps, right_back, out, stacked, spec, gathered, cat, first, second, sem, *, factor):
    copy = pltpu.make_async_copy(message.at[:, pl.ds(0, spec.shape[1])], spec, sem.at[0])
    copy.start()
    sources, length, _ = spec.shape
    block = length // 2
    coils = maps.shape[0] // 2
    rows = maps.shape[1]
    width = maps.shape[2]
    cols = width // sources
    stride = gathered.shape[0] // coils
    halo = (rows - out.shape[0]) // 2
    if stride > rows:
        gathered[...] = jnp.zeros(gathered.shape, f32)
    copy.wait()
    for s in range(sources):
        values = spec[s].astype(f32)
        for part in range(2):
            for coil in range(coils):
                to = part * width + s * cols
                gathered[coil * stride : coil * stride + rows, to : to + cols] = values[
                    part * block : part * block + rows, coil * cols : (coil + 1) * cols
                ]
    full = mm(gathered[...].astype(bf16), right_back[...])
    total = jnp.zeros((rows, 2 * width), f32)
    for coil in range(coils):
        cat[:, :width] = maps[2 * coil].astype(f32)
        cat[:, width:] = maps[2 * coil + 1].astype(f32)
        real, imag = map_pair(cat[...])
        values = full[coil * stride : coil * stride + rows]
        total = total + real * values - imag * swap(values)
    total = total * (1.0 / factor**2)
    cat[...] = total
    out[...] = cat[halo : halo + out.shape[0]]
    stack_rows(total, first, second, stacked)


class Fetch:
    def __init__(self, far, near, sems):
        self.copies = [pltpu.make_async_copy(f, n, sems.at[k]) for k, (f, n) in enumerate(zip(far, near))]
        self.near = near
        self.got = [False] * len(near)
        for copy in self.copies:
            copy.start()

    def __getitem__(self, k):
        if not self.got[k]:
            self.copies[k].wait()
            self.got[k] = True
        return self.near[k]


def apply_coils(vector, maps, mask2, right_forward, right_back, left, factor):
    total = jnp.zeros(vector.shape, f32)
    other = swap(vector)
    for coil, cat in enumerate(maps):
        real, imag = map_pair(cat()[...].astype(f32))
        sent = (real * vector + imag * other).astype(bf16)
        step = mm(sent, right_forward()[...]).astype(bf16)
        step = left_dft(left()[...], step, False) * mask2()[...].astype(f32)
        step = left_dft(left()[...], step.astype(bf16), True).astype(bf16)
        step = mm(step, right_back()[...])
        total = total + real * step - imag * swap(step)
    return total * (1.0 / factor**4)


def dot_all(a, b):
    return jnp.sum(a * b)


def operator_of(fetch, at, coils, factor):
    tables = [lambda k=k: fetch[k] for k in range(at, at + coils + 4)]
    forward, left, mask2, back = tables[0], tables[2], tables[3], tables[4]
    maps = [tables[1]] + tables[5:]
    return lambda vector: apply_coils(vector, maps, mask2, forward, back, left, factor)


def solve_first_kernel(*refs, coils, factor):
    n = coils + 5
    fetch = Fetch(refs[:n], refs[n + 1 : 2 * n + 1], refs[2 * n + 1])
    out = refs[n]
    out[...] = operator_of(fetch, 1, coils, factor)(fetch[0][...].astype(f32)).astype(bf16)


def first_step(right, applied, penalty):
    b = right.astype(f32)
    q0 = applied.astype(f32) + penalty * b
    rr0 = dot_all(b, b)
    pq0 = dot_all(b, q0)
    alpha0 = rr0 / pq0
    r1 = b - alpha0 * q0
    rn0 = dot_all(r1, r1)
    ratio0 = rn0 / rr0
    p1 = r1 + ratio0 * b
    return b, q0, rr0, pq0, alpha0, r1, rn0, ratio0, p1


def solve_second_kernel(penalty, *refs, coils, factor):
    n = coils + 6
    fetch = Fetch(refs[:n], refs[n + 1 : 2 * n + 1], refs[2 * n + 1])
    out = refs[n]
    p1 = first_step(fetch[0][...], fetch[1][...], penalty[0])[-1]
    out[...] = operator_of(fetch, 2, coils, factor)(p1).astype(bf16)


def solve_back_kernel(penalty, count, own, valid_rows, valid_cols, *refs, coils, factor):
    n = coils + 8
    fetch = Fetch(refs[:n], refs[n + 2 : 2 * n + 2], refs[2 * n + 2])
    out, scalars = refs[n : n + 2]
    tall = refs[2 * n + 3]
    lam = penalty[0]
    b, q0, rr0, pq0, alpha0, r1, rn0, ratio0, p1 = first_step(fetch[0][...], fetch[1][...], lam)
    q1 = fetch[2][...].astype(f32) + lam * p1
    pq1 = dot_all(p1, q1)
    alpha1 = rn0 / pq1
    x = alpha0 * b + alpha1 * p1
    difference = valid_rows[...] * valid_cols[...] * (x - fetch[3][...].astype(f32))
    loss = dot_all(difference, difference) / count[0]
    gx = difference * (2.0 / count[0])
    ga1 = dot_all(gx, p1)
    gpq1 = -ga1 * alpha1 / pq1
    gp = alpha1 * gx + (2.0 * gpq1) * q1
    pen = gpq1 * dot_all(p1, p1)
    grr1 = ga1 / pq1
    d1 = dot_all(gp, b)
    d2 = dot_all(gx, b)
    d4 = dot_all(gp, q0)
    d5 = dot_all(r1, q0)
    grn = grr1 + d1 / rr0
    ga = d2 - d4 - 2.0 * grn * d5
    gr = gp + (2.0 * grn) * r1
    gpq = -ga * alpha0 / pq0
    gq = gpq * b - alpha0 * gr
    grr = ga / pq0 - d1 * rn0 / (rr0 * rr0)
    pen = pen + dot_all(gq, b)
    rest = gr + ratio0 * gp + alpha0 * gx + gpq * q0 + (2.0 * grr) * b + lam * gq
    devices, window, wide = out.shape
    height = rest.shape[0]
    rows = height // devices
    pad = (tall.shape[1] - height) // 2
    for k, values in enumerate((rest, operator_of(fetch, 4, coils, factor)(gq))):
        tall[k, :pad] = jnp.zeros((pad, wide), f32)
        tall[k, pad + height :] = jnp.zeros((pad, wide), f32)
        tall[k, pad : pad + height] = values
    for d in range(devices):
        first = pad + d * rows - (window - rows) // 2
        mine = jnp.where(own[0] == d, 1.0, 0.0)
        out[d] = (tall[1, first : first + window] + mine * tall[0, first : first + window]).astype(bf16)
    lane = lax.broadcasted_iota(jnp.int32, scalars.shape, 1)
    scalars[...] = jnp.where(lane == 0, loss, jnp.where(lane == 1, pen, 0.0))


def grad_denoised_kernel(windows, denoised, penalty, stacked, scalars, cat, first, second):
    total = jnp.sum(windows[...].astype(f32), axis=0)
    cat[...] = total
    reach = (cat.shape[0] - denoised.shape[0]) // 2
    pen = dot_all(cat[reach : reach + denoised.shape[0]], denoised[...])
    scalars[...] = jnp.full(scalars.shape, pen, f32)
    stack_rows(penalty[0] * total, first, second, stacked)


def per_channel(row):
    turned = jnp.transpose(jnp.broadcast_to(row, (128, 128)))
    tiled = jnp.concatenate([turned] * (LANES // 128), axis=1)
    return tiled[:CH], tiled[CH:]


def gathered_sums(stats):
    values = stats[...]
    row = lax.broadcasted_iota(jnp.int32, values.shape, 0) % 2
    sums = jnp.sum(jnp.where(row == 0, values, 0.0), axis=0, keepdims=True)
    counts = jnp.sum(jnp.where(row == 1, values, 0.0), axis=0, keepdims=True)
    return sums, counts[:, :1]


def norm_terms(stats, gain_bias, layer):
    sums, count = gathered_sums(stats)
    means = sums / count
    average, second = per_channel(means)
    rstd = lax.rsqrt(second - average * average + norm_epsilon)
    gain, bias = per_channel(gain_bias[layer])
    return average, rstd, gain, bias


def fold(values):
    return sum(values[:, 128 * t : 128 * (t + 1)] for t in range(LANES // 128))


def write_sums(out, acc1, acc2, extra):
    both = jnp.concatenate([acc1, acc2], axis=0)
    row = jnp.sum(jnp.transpose(both), axis=0, keepdims=True)
    second = jnp.broadcast_to(extra, row.shape)
    which = lax.broadcasted_iota(jnp.int32, out.shape, 0) % 2
    out[...] = jnp.where(which == 0, row, second)


def plan(count):
    for rows in (10, 12, 11, 13, 14, 9, 8):
        if count % rows == 0:
            return rows, count // rows, 0
    if count <= 14:
        return count, 1, 0
    return 10, count // 10, count % 10


class Rows:
    def __init__(self, hbm, vmem, sems, count, base=0, lead=0, inward=True):
        self.hbm, self.vmem, self.sems = hbm, vmem, sems
        self.count, self.base, self.lead, self.inward = count, base, lead, inward
        self.rows, self.whole, self.rest = plan(count)

    def copy(self, at, rows, slot):
        far = self.hbm.at[pl.ds(at + self.base, rows)]
        near = self.vmem.at[pl.ds(at, rows)]
        if self.inward:
            return pltpu.make_async_copy(far, near, self.sems.at[slot])
        return pltpu.make_async_copy(near, far, self.sems.at[slot])

    def block(self, t, rows):
        return self.copy(t * self.rows + self.lead, rows, t)

    def head(self):
        return self.copy(0, self.lead, self.whole + 1)

    def each(self, action):
        def one(t, carry):
            action(self.block(t, self.rows))
            return carry

        lax.fori_loop(0, self.whole, one, 0)
        if self.rest:
            action(self.block(self.whole, self.rest))

    def start(self):
        if self.lead:
            self.head().start()
        self.each(lambda copy: copy.start())

    def wait(self):
        self.each(lambda copy: copy.wait())


def over_rows(count, step, carry):
    rows, whole, rest = plan(count)
    carry = lax.fori_loop(0, whole, lambda t, state: step(t, t * rows, rows, state), carry)
    if rest:
        carry = step(whole, whole * rows, rest, carry)
    return carry


def sems(count):
    return pltpu.SemaphoreType.DMA((plan(count)[1] + 2,))


def plane(dtype, rows):
    return pltpu.VMEM((rows, CH, LANES), dtype)


def zero_sums():
    return jnp.zeros((CH, 128), f32), jnp.zeros((CH, 128), f32)


def beside(values):
    return values[0] if len(values) == 1 else jnp.concatenate(values, axis=1)


def lanes_of(values, u):
    return values[:, u * LANES : (u + 1) * LANES]


def taps_sum(y):
    n = y.shape[0] // 3
    return pltpu.roll(y[:n], 1, 1) + y[n : 2 * n] + pltpu.roll(y[2 * n :], LANES - 1, 1)


def taps(rows8):
    return jnp.concatenate([pltpu.roll(rows8, 1, 1), rows8, pltpu.roll(rows8, LANES - 1, 1)], axis=0).astype(bf16)


def first_conv_kernel(stacked, weight, mask, count, out_hbm, sums, out, out_sems):
    n = out.shape[0]
    at = (mask.shape[0] - n) // 2
    store = Rows(out_hbm, out, out_sems, n, inward=False)
    w = weight[...]

    def step(t, r0, rows, acc):
        y = mm(w, beside([taps(stacked[r0 + u]) for u in range(rows)]))
        for u in range(rows):
            value = lanes_of(y, u)
            out[r0 + u] = value.astype(bf16)
            kept = value * mask[pl.ds(r0 + u + at, 1), :]
            acc = acc[0] + fold(kept), acc[1] + fold(kept * value)
        store.block(t, rows).start()
        return acc

    acc = over_rows(n, step, zero_sums())
    write_sums(sums, *acc, count[0])
    store.wait()


def activation(hidden, stats, gain_bias, layer, inside, at):
    average, rstd, gain, bias = norm_terms(stats, gain_bias, layer)
    scale = gain * rstd
    shift = bias - average * scale

    def activate(r):
        return (jnp.maximum(hidden[r].astype(f32) * scale + shift, 0.0) * inside[pl.ds(r + at, 1), :]).astype(bf16)

    return activate


def three_rows(values):
    return beside([jnp.concatenate(values[u : u + 3], axis=0) for u in range(len(values) - 2)])


def conv_kernel(
    hidden_hbm, stats, gain_bias, weight, inside, mask, count, out_hbm, sums, hidden, out, in_sems, out_sems, *, layer
):
    n = out.shape[0]
    at = (mask.shape[0] - n) // 2
    load = Rows(hidden_hbm, hidden, in_sems, n, lead=2)
    store = Rows(out_hbm, out, out_sems, n, inward=False)
    load.start()
    activate = activation(hidden, stats, gain_bias, layer, inside, at - 1)
    w = weight[layer]
    load.head().wait()

    def step(t, r0, rows, acc):
        load.block(t, rows).wait()
        y = mm(w, three_rows([activate(r0 + u) for u in range(rows + 2)]))
        for u in range(rows):
            value = taps_sum(lanes_of(y, u))
            out[r0 + u] = value.astype(bf16)
            kept = value * mask[pl.ds(r0 + u + at, 1), :]
            acc = acc[0] + fold(kept), acc[1] + fold(kept * value)
        store.block(t, rows).start()
        return acc

    acc = over_rows(n, step, zero_sums())
    write_sums(sums, *acc, count[0])
    store.wait()


def last_conv_kernel(
    hidden_hbm, stats, gain_bias, weight, inside, initial, penalty, denoised, right, hidden, branch, in_sems, *, base
):
    n, wide = branch.shape
    width = wide // 2
    load = Rows(hidden_hbm, hidden, in_sems, n, base=base, lead=2)
    load.start()
    activate = activation(hidden, stats, gain_bias, 3, inside, HALO - 1)
    w = weight[...]
    load.head().wait()

    def step(t, r0, rows, carry):
        load.block(t, rows).wait()
        y = mm(w, three_rows([activate(r0 + u) for u in range(rows + 2)]))
        for u in range(rows):
            value = taps_sum(lanes_of(y, u))
            branch[pl.ds(r0 + u, 1), :width] = value[0:1, :width]
            branch[pl.ds(r0 + u, 1), width:] = value[1:2, :width]
        return carry

    over_rows(n, step, 0)
    sent = initial[...]
    result = sent + branch[...]
    denoised[...] = result
    sent = (sent + penalty[0] * result).astype(bf16)
    for d in range(right.shape[0]):
        right[d] = sent


def moments_kernel(hidden_hbm, stats, gain_bias, mask, stacked, out, hidden, in_sems, *, base, stack_base):
    n = hidden.shape[0]
    load = Rows(hidden_hbm, hidden, in_sems, n, base=base)
    load.start()
    average, rstd, _, _ = norm_terms(stats, gain_bias, 0)
    out[...] = jnp.zeros(out.shape, f32)

    def step(t, r0, rows, carry):
        load.block(t, rows).wait()
        left = []
        for u in range(rows):
            valid = jnp.broadcast_to(mask[pl.ds(r0 + u + HALO, 1), :], (8, LANES))
            normed = (hidden[r0 + u].astype(f32) - average) * rstd * mask[pl.ds(r0 + u + HALO, 1), :]
            left.append(jnp.concatenate([normed, valid], axis=0).astype(bf16))
        out[...] += outer(beside(left), beside([taps(stacked[r0 + stack_base + u]) for u in range(rows)]))
        return carry

    over_rows(n, step, 0)


def grad_tail(ga, hidden_row, terms, inside_row):
    average, rstd, gain, bias = terms
    normed = (hidden_row.astype(f32) - average) * rstd
    keep = (gain * normed + bias > 0.0) & (inside_row > 0.0)
    return jnp.where(keep, ga, 0.0), normed


def back_last_kernel(
    stacked, weight, hidden_hbm, stats, gain_bias, inside, own, gy_hbm, sums, hidden, gy, in_sems, out_sems
):
    n = gy.shape[0]
    at = (inside.shape[0] - n) // 2
    load = Rows(hidden_hbm, hidden, in_sems, n)
    store = Rows(gy_hbm, gy, out_sems, n, inward=False)
    load.start()
    terms = norm_terms(stats, gain_bias, 3)
    w = weight[...]

    def step(t, r0, rows, acc):
        load.block(t, rows).wait()
        y = mm(w, beside([taps(stacked[r0 + u]) for u in range(rows)]))
        for u in range(rows):
            value, normed = grad_tail(lanes_of(y, u), hidden[r0 + u], terms, inside[pl.ds(r0 + u + at, 1), :])
            gy[r0 + u] = value.astype(bf16)
            kept = value * own[pl.ds(r0 + u + at, 1), :]
            acc = acc[0] + fold(kept), acc[1] + fold(kept * normed)
        store.block(t, rows).start()
        return acc

    acc = over_rows(n, step, zero_sums())
    write_sums(sums, *acc, 0.0)
    store.wait()


def hidden_grad_terms(stats, back_stats, gain_bias, layer):
    average, rstd, gain, _ = norm_terms(stats, gain_bias, layer)
    _, count = gathered_sums(stats)
    back, _ = gathered_sums(back_stats)
    s1, s2 = per_channel(back / count)
    return average, rstd, gain * rstd, s1, s2


def back_kernel(
    gy_in_hbm, hidden_in_hbm, stats_in, back_stats, gain_bias, mask,
    weight, hidden_hbm, stats, inside, own, *rest, layer
):
    final = layer == 1
    skip_in, skip = 6 - 2 * layer, 8 - 2 * layer
    if final:
        stacked, cross, grad_hbm, sums = rest[0], rest[1], rest[2], rest[3]
        gy_in, hidden_in, hidden, grad, s_gy, s_hin, s_hid, s_grad = rest[4:]
        stack_base = (stacked.shape[0] - hidden.shape[0]) // 2
    else:
        grad_hbm, gy_hbm, sums = rest[0], rest[1], rest[2]
        gy_in, hidden_in, hidden, grad, gy, s_gy, s_hin, s_hid, s_grad, s_out = rest[3:]
    n = hidden.shape[0]
    at = (inside.shape[0] - n) // 2
    load_gy = Rows(gy_in_hbm, gy_in, s_gy, n, lead=2)
    load_in = Rows(hidden_in_hbm, hidden_in, s_hin, n, base=skip_in, lead=2)
    load = Rows(hidden_hbm, hidden, s_hid, n, base=skip)
    store_grad = Rows(grad_hbm, grad, s_grad, n, lead=2, inward=False)
    for group in (load_gy, load_in, load):
        group.start()
    average, rstd, scale, s1, s2 = hidden_grad_terms(stats_in, back_stats, gain_bias, layer)
    terms = norm_terms(stats, gain_bias, layer - 1)
    w = weight[layer - 1]

    def hidden_grad(r):
        normed = (hidden_in[r].astype(f32) - average) * rstd
        return (scale * (gy_in[r].astype(f32) - mask[pl.ds(r + at - 1, 1), :] * (s1 + normed * s2))).astype(bf16)

    load_gy.head().wait()
    load_in.head().wait()
    for r in range(2):
        grad[r] = hidden_grad(r)
    store_grad.head().start()
    if final:
        cross[...] = jnp.zeros(cross.shape, f32)
    else:
        store = Rows(gy_hbm, gy, s_out, n, inward=False)

    def step(t, r0, rows, acc):
        load_gy.block(t, rows).wait()
        load_in.block(t, rows).wait()
        load.block(t, rows).wait()
        grads = [hidden_grad(r0 + u) for u in range(rows + 2)]
        for u in range(2, rows + 2):
            grad[r0 + u] = grads[u]
        store_grad.block(t, rows).start()
        y = mm(w, three_rows(grads))
        values = []
        for u in range(rows):
            value, normed = grad_tail(taps_sum(lanes_of(y, u)), hidden[r0 + u], terms, inside[pl.ds(r0 + u + at, 1), :])
            kept = value * own[pl.ds(r0 + u + at, 1), :]
            acc = acc[0] + fold(kept), acc[1] + fold(kept * normed)
            if final:
                values.append(value.astype(bf16))
            else:
                gy[r0 + u] = value.astype(bf16)
        if final:
            cross[...] += outer(beside(values), beside([taps(stacked[r0 + stack_base + u]) for u in range(rows)]))
        else:
            store.block(t, rows).start()
        return acc

    acc = over_rows(n, step, zero_sums())
    write_sums(sums, *acc, 0.0)
    store_grad.head().wait()
    store_grad.wait()
    if not final:
        store.wait()


def shifted(row):
    wide = row.astype(f32)
    return jnp.concatenate(
        [pltpu.roll(wide, LANES - 1, 1).astype(bf16), row, pltpu.roll(wide, 1, 1).astype(bf16)], axis=0
    )


def outer(a, b):
    return lax.dot_general(a, b, (((1,), (1,)), ((), ())), preferred_element_type=f32)


def weight_grad_kernel(
    grad_hbm, hidden_hbm, stats, gain_bias, inside, out, grad, hidden, s_grad, s_hid, *, layer
):
    n = grad.shape[0]
    load_grad = Rows(grad_hbm, grad, s_grad, n, base=layer)
    load = Rows(hidden_hbm, hidden, s_hid, n, base=6 - layer, lead=2)
    load.start()
    load_grad.start()
    activate = activation(hidden, stats, gain_bias, layer - 1, inside, HALO - 1)
    out[...] = jnp.zeros(out.shape, f32)
    load.head().wait()

    def step(t, r0, rows, carry):
        load.block(t, rows).wait()
        load_grad.block(t, rows).wait()
        left = beside([shifted(grad[r0 + u]) for u in range(rows)])
        right = three_rows([activate(r0 + u) for u in range(rows + 2)])
        out[...] += outer(left, right)
        return carry

    over_rows(n, step, 0)


def last_weight_grad_kernel(stacked, hidden_hbm, stats, gain_bias, inside, out, hidden, in_sems, *, base, stack_base):
    n = hidden.shape[0]
    load = Rows(hidden_hbm, hidden, in_sems, n, base=base)
    load.start()
    activate = activation(hidden, stats, gain_bias, 3, inside, HALO)
    out[...] = jnp.zeros(out.shape, f32)

    def step(t, r0, rows, carry):
        load.block(t, rows).wait()
        left = beside([activate(r0 + u) for u in range(rows)])
        out[...] += outer(left, beside([taps(stacked[r0 + stack_base + u]) for u in range(rows)]))
        return carry

    over_rows(n, step, 0)


def spread(values, axes, size):
    wide = jnp.broadcast_to(values[None], (size,) + values.shape).reshape((size * values.shape[0],) + values.shape[1:])
    return lax.all_to_all(wide, axes, 0, 0, tiled=True)


def row_shift(values, hops):
    size = lax.axis_size("img")
    pairs = [(i, i + hops) for i in range(size) if 0 <= i + hops < size]
    return lax.ppermute(values, "img", pairs)


def with_halo(values, width):
    rows = values.shape[1]
    before, after = [], []
    need, hop = width, 1
    while need > 0:
        part = min(need, rows)
        before.insert(0, row_shift(values[:, rows - part :], hop))
        after.append(row_shift(values[:, :part], -hop))
        need -= part
        hop += 1
    return jnp.concatenate(before + [values] + after, axis=1)


def tap_weights(values):
    values = values.reshape(CH, 3, 3, 2).transpose(0, 2, 1, 3).reshape(CH, 3, 6)
    return jnp.pad(values, ((0, 0), (0, 0), (0, 2))).reshape(CH, 24)


def adamw(weight, grad, first_m, second_m, rate, decay, step_value):
    mean_new = beta_one * first_m + (1.0 - beta_one) * grad
    square_new = beta_two * second_m + (1.0 - beta_two) * grad * grad
    mean_hat = mean_new / (1.0 - beta_one**step_value)
    square_hat = square_new / (1.0 - beta_two**step_value)
    updated = weight - rate * (mean_hat / (jnp.sqrt(square_hat) + adam_epsilon) + decay * weight)
    return (updated, mean_new, square_new)


def body(
    kspace_data, coil_maps, sample_mask, valid_mask, target,
    first_weight, middle_weights, last_weight, norm_params, penalty,
    first_mean, first_square, middle_mean, middle_square, last_mean, last_square,
    norm_mean, norm_square, penalty_mean, penalty_square, step_count,
):
    n_img = lax.axis_size("img")
    n_ch = lax.axis_size("ch")
    n_all = n_img * n_ch
    own_ch = lax.axis_index("ch")
    own_img = lax.axis_index("img")
    coils = kspace_data.shape[1]
    height = kspace_data.shape[3]
    width = coil_maps.shape[4]
    rows = coil_maps.shape[3]
    cols = kspace_data.shape[4]
    wide = 2 * width
    per_dev = -(-coils // n_img)
    right_forward, right_back, left, factor = dft_tables(width)

    window = rows + 2 * HALO
    block = rup(window, 8)
    half = rup(coils * cols, 128)
    at_maps = 2 * block
    length = at_maps + (per_dev + 1) * rows
    valid_own = lax.dynamic_index_in_dim(valid_mask, own_ch, 0, keepdims=False).astype(f32)
    any_rows = jnp.max(valid_own, 1).astype(bf16)[None]
    any_cols = jnp.max(valid_own, 0).astype(bf16).reshape(2, width // 2)
    (message,) = call(
        lambda *refs: message_kernel(*refs, at_maps=at_maps), [VM] * 7, [((n_img, length, wide), bf16, VM)],
        (kspace_data[0].transpose(0, 1, 3, 2), sample_mask[0].T, coil_maps[0], target[0], any_rows, any_cols, left),
        scratch=[pltpu.VMEM((2 * half, height), f32), pltpu.VMEM((height + 16, 2 * half), f32)], name="message",
    )

    packed = jnp.concatenate(
        [middle_weights.reshape(-1), first_weight.reshape(-1), last_weight.reshape(-1), norm_params.reshape(-1)]
    )
    packed = jnp.pad(packed, (0, rup(packed.size, 1024) - packed.size)).reshape(-1, 128)
    planes = coil_maps[0].reshape(2 * coils, rows, width).astype(bf16)
    message, packed, planes = lax.optimization_barrier((message, packed, planes))
    message = lax.all_to_all(message, "img", 0, 0, tiled=True)
    everyone = jnp.zeros((n_ch,) + packed.shape, f32)
    for hop in range(n_ch):
        came = packed if hop == 0 else lax.ppermute(packed, "ch", [(i, (i + hop) % n_ch) for i in range(n_ch)])
        everyone = lax.dynamic_update_index_in_dim(everyone, came, (own_ch - hop) % n_ch, 0)
    tall_maps = with_halo(planes, HALO)
    initial, stacked = call(
        lambda *refs: initial_kernel(*refs, factor=factor), [HB, VM, VM],
        [((rows, wide), f32, VM), ((window - 2, 8, LANES), f32, VM)],
        (message, tall_maps, right_back),
        scratch=[
            pltpu.VMEM((n_img, at_maps, wide), bf16), pltpu.VMEM((coils * rup(window, 8), wide), f32),
            pltpu.VMEM((window, wide), f32), pltpu.VMEM((window, LANES), f32), pltpu.VMEM((window, LANES), f32),
            pltpu.SemaphoreType.DMA((1,)),
        ],
        name="initial",
    )

    sizes = [middle_weights.size, first_weight.size, last_weight.size, norm_params.size]
    cuts = np.cumsum([0] + sizes)
    shapes = [middle_weights.shape, first_weight.shape, last_weight.shape, norm_params.shape]
    channel_dim = [2, 1, 2, 2]

    def full(k):
        piece = everyone.reshape(n_ch, -1)[:, cuts[k] : cuts[k + 1]].reshape((n_ch,) + shapes[k])
        piece = jnp.moveaxis(piece, 0, channel_dim[k])
        dims = list(shapes[k])
        dims[channel_dim[k]] *= n_ch
        return piece.reshape(dims)

    middle_all, first_all, last_all, norms_all = (full(k) for k in range(4))
    low = middle_all.astype(bf16).reshape(3, 3, 3, CH, CH)
    forward_w = low.transpose(0, 2, 3, 1, 4).reshape(3, 3 * CH, 3 * CH)
    back_w = low[:, ::-1, ::-1].transpose(0, 2, 4, 1, 3).reshape(3, 3 * CH, 3 * CH)
    first_w = tap_weights(first_all.astype(bf16).transpose(1, 0, 2))
    last_low = last_all.astype(bf16)
    last_w = last_low.reshape(3, 3, 2, CH).transpose(1, 2, 0, 3)
    last_w = jnp.pad(last_w, ((0, 0), (0, 6), (0, 0), (0, 0))).reshape(24, 3 * CH)
    last_back_w = tap_weights(last_low[::-1].transpose(2, 0, 1))
    gain_bias = norms_all.reshape(4, 1, 2 * CH)

    row_at = own_img * rows - HALO + jnp.arange(rows + 2 * HALO)
    in_image = ((row_at >= 0) & (row_at < height)).astype(f32)
    in_lane = (jnp.arange(LANES) < width).astype(f32)
    inside = in_image[:, None] * in_lane[None, :]
    is_own = ((row_at >= own_img * rows) & (row_at < (own_img + 1) * rows)).astype(f32)
    own_valid = jnp.pad(valid_own, ((HALO, HALO), (0, LANES - width)))
    own_lane = is_own[:, None] * in_lane[None, :]
    local_count = jnp.sum(valid_own)[None]

    def exchange(values):
        return lax.all_to_all(values, BOTH, 0, 0, tiled=True)

    sums_out = ((2 * n_all, 128), f32, VM)

    def hidden_out(reach):
        return ((rows + 2 * reach, CH, LANES), bf16, HB)

    out, sums = call(
        first_conv_kernel, [VM, VM, VM, SM], [hidden_out(6), sums_out],
        (stacked, first_w, own_valid, local_count),
        scratch=[plane(bf16, rows + 12), sems(rows + 12)], name="conv1",
    )
    hidden = [out]
    stats = [exchange(sums)]
    for layer in range(3):
        n = rows + 10 - 2 * layer
        out, sums = call(
            lambda *refs: conv_kernel(*refs, layer=layer), [HB] + [VM] * 5 + [SM], [hidden_out(5 - layer), sums_out],
            (hidden[layer], stats[layer], gain_bias, forward_w, inside, own_valid, local_count),
            scratch=[plane(bf16, n + 2), plane(bf16, n), sems(n), sems(n)], name=f"conv{layer + 2}",
        )
        hidden.append(out)
        stats.append(exchange(sums))
    denoised, right = call(
        lambda *refs: last_conv_kernel(*refs, base=2), [HB] + [VM] * 5 + [SM],
        [((rows, wide), f32, VM), ((n_img, rows, wide), bf16, VM)],
        (hidden[3], stats[3], gain_bias, last_w, inside, initial, penalty),
        scratch=[plane(bf16, rows + 2), pltpu.VMEM((rows, wide), f32), sems(rows)], name="conv5",
    )

    pieces = [
        message[:, at_maps + c * rows : at_maps + (c + 1) * rows].reshape(height, wide) for c in range(per_dev + 1)
    ]
    maps_full, target_full = pieces[:per_dev], pieces[per_dev]
    flags = message[:, : 2 * block, wide - width // 2 :].reshape(n_img, 2, block, width // 2)
    turned = jnp.concatenate([flags[:, p, :cols].reshape(width, width // 2).T for p in range(2)], axis=0)
    mask2 = jnp.concatenate([turned, turned], axis=1)
    rest = flags[:, 1, cols:].astype(f32)
    valid_cols = jnp.max(rest[:, :2], axis=0).reshape(width)
    valid_rows = rest[:, 2, :rows].reshape(height)
    near_rows = lax.dynamic_slice_in_dim(jnp.pad(valid_rows, (HALO, HALO)), own_img * rows, rows + 2 * HALO, 0)
    valid_near = near_rows[:, None] * jnp.pad(valid_cols, (0, LANES - width))[None, :]
    valid_rows = valid_rows[:, None]
    valid_cols = jnp.concatenate([valid_cols, valid_cols])[None, :]
    operator_args = [right_forward, maps_full[0], left, mask2, right_back] + maps_full[1:]

    def send(values):
        return lax.all_to_all(values, "img", 0, 0, tiled=True)

    def solve(kernel, scalars, vmem, arrays, outs, name, extra=()):
        arrays = list(arrays) + operator_args
        return call(
            lambda *refs: kernel(*refs, coils=per_dev, factor=factor), [SM] * len(scalars) + [VM] * len(vmem) + [HB] * len(arrays), outs,
            (*scalars, *vmem, *arrays),
            scratch=[pltpu.VMEM(a.shape, a.dtype) for a in arrays] + [pltpu.SemaphoreType.DMA((len(arrays),))] + list(extra),
            name=name,
        )

    def gathered(partial):
        got = send(partial.reshape(n_img, rows, wide))
        total = jnp.sum(got.astype(f32), axis=0).astype(bf16)
        return send(jnp.broadcast_to(total[None], (n_img, rows, wide))).reshape(height, wide)

    whole = ((height, wide), bf16, VM)
    right = send(right).reshape(height, wide)
    (partial,) = solve(solve_first_kernel, (), (), (right,), [whole], "solve1")
    applied0 = gathered(partial)
    (partial,) = solve(solve_second_kernel, (penalty,), (), (right, applied0), [whole], "solve2")
    applied1 = gathered(partial)
    count = jnp.sum(stats[0][1::2, 0])[None]
    (moments,) = call(
        lambda *refs: moments_kernel(*refs, base=6, stack_base=6), [HB] + [VM] * 4, [((CH + 8, 24), f32, VM)],
        (hidden[0], stats[0], gain_bias, own_valid, stacked),
        scratch=[plane(bf16, rows), sems(rows)], name="moments",
    )
    tall_rows = rows + 8
    windows, scalars = solve(
        solve_back_kernel, (penalty, count, own_img.astype(jnp.int32)[None]), (valid_rows, valid_cols),
        (right, applied0, applied1, target_full),
        [((n_img, tall_rows, wide), bf16, VM), ((8, 128), f32, VM)], "solve3",
        extra=[pltpu.VMEM((2, height + 16, wide), f32)],
    )
    windows = send(windows)
    windows, moments = lax.optimization_barrier((windows, moments))
    grad_stack, pen_own = call(
        grad_denoised_kernel, [VM, VM, SM], [((rows + 6, 8, LANES), f32, VM), ((8, 128), f32, VM)],
        (windows, denoised, penalty),
        scratch=[
            pltpu.VMEM((tall_rows, wide), f32), pltpu.VMEM((tall_rows, LANES), f32), pltpu.VMEM((tall_rows, LANES), f32),
        ],
        name="grad_denoised",
    )
    pen_part = scalars[0, 1] / n_img + pen_own[0, 0]
    loss_part = scalars[0, 0] / n_img

    n = rows + 6
    gy, sums = call(
        back_last_kernel, [VM, VM, HB] + [VM] * 4, [hidden_out(3), sums_out],
        (grad_stack, last_back_w, hidden[3], stats[3], gain_bias, inside, own_lane),
        scratch=[plane(bf16, n), plane(bf16, n), sems(n), sems(n)], name="back5",
    )
    back_stats = [None] * 4
    back_stats[3] = exchange(sums)
    (grad_last,) = call(
        lambda *refs: last_weight_grad_kernel(*refs, base=3, stack_base=3),
        [VM, HB] + [VM] * 3, [((CH, 24), f32, VM)],
        (grad_stack, hidden[3], stats[3], gain_bias, inside),
        scratch=[plane(bf16, rows), sems(rows)], name="wgrad5",
    )
    back_stats[3], grad_last = lax.optimization_barrier((back_stats[3], grad_last))
    grad_middle = [None] * 3
    cross = None
    for layer in (3, 2, 1):
        n = rows + 2 * layer - 2
        final = layer == 1
        ins = [HB, HB] + [VM] * 5 + [HB] + [VM] * 3
        args = (
            gy, hidden[layer], stats[layer], back_stats[layer], gain_bias, valid_near,
            back_w, hidden[layer - 1], stats[layer - 1], inside, own_lane,
        )
        scratch = [plane(bf16, n + 2), plane(bf16, n + 2), plane(bf16, n), plane(bf16, n + 2)]
        kernel = lambda *refs: back_kernel(*refs, layer=layer)
        if final:
            cross, grad, sums = call(
                kernel, ins + [VM], [((CH, 24), f32, VM), hidden_out(layer), sums_out], args + (stacked,),
                scratch=scratch + [sems(n)] * 4, name="back2",
            )
        else:
            grad, gy, sums = call(
                kernel, ins, [hidden_out(layer), hidden_out(layer - 1), sums_out], args,
                scratch=scratch + [plane(bf16, n)] + [sems(n)] * 5, name=f"back{layer + 1}",
            )
            back_stats[layer - 1] = exchange(sums)
        (grad_middle[layer - 1],) = call(
            lambda *refs: weight_grad_kernel(*refs, layer=layer),
            [HB, HB] + [VM] * 3, [((3 * CH, 3 * CH), f32, VM)],
            (grad, hidden[layer - 1], stats[layer - 1], gain_bias, inside),
            scratch=[plane(bf16, rows), plane(bf16, rows + 2), sems(rows), sems(rows)], name=f"wgrad{layer + 1}",
        )
        if not final:
            back_stats[layer - 1], grad_middle[layer - 1] = lax.optimization_barrier(
                (back_stats[layer - 1], grad_middle[layer - 1])
            )

    own = CH // n_ch
    sums_row = sums[0]
    small = jnp.concatenate(
        [
            cross, grad_last, moments[:CH], sums_row[:CH, None], sums_row[CH:, None],
            jnp.full((CH, 1), loss_part), jnp.full((CH, 1), pen_part), jnp.zeros((CH, 4), f32),
            jnp.broadcast_to(moments[CH : CH + 1], (CH, 24)), jnp.zeros((CH, 24), f32),
        ],
        axis=1,
    )
    small = jnp.broadcast_to(small.reshape(1, n_ch, own, 128), (n_img, n_ch, own, 128)).reshape(n_all, own, 128)
    share = 27 * own * CH // n_img
    lane = 128 if share % 128 == 0 else share
    middle = jnp.stack(grad_middle).reshape(3, 3, n_ch, n_img, own * CH * 3 // n_img)
    if own % n_img == 0:
        blocks = middle.transpose(3, 2, 0, 1, 4)
    else:
        blocks = jnp.stack(grad_middle).reshape(9, n_ch, own * 3 * CH).transpose(1, 0, 2)
        blocks = blocks.reshape(n_ch, n_img, share).transpose(1, 0, 2)
    blocks = blocks.reshape(n_all, share // lane, lane)
    if lane == 128:
        got = exchange(jnp.concatenate([small, blocks], axis=1))
        total = jnp.sum(got.reshape(n_all, own + share // 128, 128), axis=0)
        small_total, mine = total[:own], total[own:]
    else:
        small_total = jnp.sum(exchange(small), axis=0)
        mine = jnp.sum(exchange(blocks), axis=0)
    mine = spread(mine, "img", n_img)
    if own % n_img == 0:
        middle_own = mine.reshape(n_img, 3, 3, own // n_img, 3, CH)
        grad_middle_own = middle_own.transpose(1, 4, 2, 0, 3, 5).reshape(middle_weights.shape)
    else:
        middle_own = mine.reshape(3, 3, own, 3, CH)
        grad_middle_own = middle_own.transpose(0, 3, 1, 2, 4).reshape(middle_weights.shape)

    means, pixels = gathered_sums_plain(stats[0])
    norms_own = lax.dynamic_slice_in_dim(norms_all, own_ch * own, own, 2)
    average = lax.dynamic_slice_in_dim(means[:CH] / pixels, own_ch * own, own, 0)
    second = lax.dynamic_slice_in_dim(means[CH:] / pixels, own_ch * own, own, 0)
    scale = norms_own[0, 0] * lax.rsqrt(second - average * average + norm_epsilon)
    s1, s2 = small_total[:, 72:73], small_total[:, 73:74]
    first_total = scale[:, None] * (
        small_total[:, :24] - (s1 * small_total[:, 80:104] + s2 * small_total[:, 48:72]) / pixels
    )

    def tap_major(values):
        return values.reshape(own, 3, 8)[:, :, :6].reshape(own, 3, 3, 2).transpose(2, 1, 0, 3).reshape(9, own, 2)

    grad_first_own = tap_major(first_total)
    grad_last_own = tap_major(small_total[:, 24:48])[::-1].transpose(0, 2, 1)
    loss_value = small_total[0, 74]
    grad_penalty = small_total[0, 75]
    later = jnp.stack([jnp.sum(s[::2], axis=0) for s in back_stats[1:]]).reshape(3, 2, CH)
    later = lax.dynamic_slice_in_dim(later, own_ch * own, own, 2)
    grad_norm_own = jnp.concatenate([jnp.stack([s1[:, 0], s2[:, 0]])[None], later], axis=0)[:, ::-1]

    step_value = step_count[0].astype(f32) + 1.0
    first_out = adamw(first_weight, grad_first_own, first_mean, first_square, rate_conv, decay_rate, step_value)
    middle_out = adamw(middle_weights, grad_middle_own, middle_mean, middle_square, rate_conv, decay_rate, step_value)
    last_out = adamw(last_weight, grad_last_own, last_mean, last_square, rate_conv, decay_rate, step_value)
    norm_out = adamw(norm_params, grad_norm_own, norm_mean, norm_square, rate_norm, 0.0, step_value)
    penalty_out = adamw(penalty, grad_penalty[None], penalty_mean, penalty_square, rate_penalty, 0.0, step_value)
    return (loss_value,) + first_out + middle_out + last_out + norm_out + (jnp.concatenate(penalty_out),)


def gathered_sums_plain(stats):
    return jnp.sum(stats[::2], axis=0), jnp.sum(stats[1::2, 0])


def solution(mesh):
    in_specs = (
        P("ch", None, None, None, "img"),
        P("ch", None, None, "img", None),
        P("ch", None, "img"),
        P(None, "img", None),
        P("ch", None, "img", None),
        P(None, "ch", None),
        P(None, None, "ch", None),
        P(None, None, "ch"),
        P(None, None, "ch"),
        P(),
        P(None, "ch", None),
        P(None, "ch", None),
        P(None, None, "ch", None),
        P(None, None, "ch", None),
        P(None, None, "ch"),
        P(None, None, "ch"),
        P(None, None, "ch"),
        P(None, None, "ch"),
        P(),
        P(),
        P(),
    )
    out_specs = (
        P(),
        P(None, "ch", None),
        P(None, "ch", None),
        P(None, "ch", None),
        P(None, None, "ch", None),
        P(None, None, "ch", None),
        P(None, None, "ch", None),
        P(None, None, "ch"),
        P(None, None, "ch"),
        P(None, None, "ch"),
        P(None, None, "ch"),
        P(None, None, "ch"),
        P(None, None, "ch"),
        P(),
    )
    return jax.shard_map(body, mesh=mesh, in_specs=in_specs, out_specs=out_specs, check_vma=False)
```

time: 553 us -> 443 us (0.80); the launches traced: 542 us -> 438 us
  Pallas kernels: 209 us -> 144 us
  local copies, waits for them, and re-layouts: 72.1 us -> 38.2 us
  blocking collectives: 47 us -> 77.9 us
  waiting for transfers between devices: 115 us -> 89.6 us
  starting transfers between devices: 73.6 us -> 61.3 us
    pallas_call x19 -> x20, Pallas kernels: 209 us -> 144 us  [call(): pl.pallas_call(kernel, out_shape=[jax.ShapeDtypeStruct(shape, dtype) for...]
    all_to_all x3 -> x5, blocking collectives: 47 us -> 77.9 us  [the longest x3 46.9 us: send(): return lax.all_to_all(values, 'img', 0, 0, tiled=True)]
    all_to_all x5 -> x1, waiting for transfers between devices: 23.2 us -> 2.57 us  [spread(): return lax.all_to_all(wide, axes, 0, 0, tiled=True)]
    unnamed x102 -> x80, local copies, waits for them, and re-layouts: 22.7 us -> 8.45 us
    all_to_all x5 -> x1, starting transfers between devices: 17.5 us -> 3.67 us  [spread(): return lax.all_to_all(wide, axes, 0, 0, tiled=True)]
    slice x50 -> x25, local copies, waits for them, and re-layouts: 18.2 us -> 8.49 us  [the longest x2 2.55 us: body(): pen_part = scalars[0, 1] / n_img + pen_own[0, 0]]
    squeeze x13 -> x0, local copies, waits for them, and re-layouts: 9.43 us -> none  [the longest x3 2.42 us: body(): back_w[layer - 1]]
    ppermute x4 -> x2, waiting for transfers between devices: 2.38 us -> 10.8 us  [row_shift(): return lax.ppermute(values, 'img', pairs)]
  transfers between devices with their start and end apart: 21 -> 16, of which waited for: 15 -> 11; matrix products, arithmetic and copies ran while one was open for 10% -> 7% of each run, Pallas kernels for 9% -> 5%
where the time goes in v2:
time: 443 us; the launch traced here: 438 us
  Pallas kernels  144 us (33%)
  waiting for transfers between devices  89.6 us (20%)
  blocking collectives  77.9 us (18%)
  starting transfers between devices  61.3 us (14%)
  local copies, waits for them, and re-layouts  38.2 us (9%)
  other arithmetic  18.3 us (4%)
  between operations  8.71 us (2%)
    pallas_call x20, Pallas kernels, call(): pl.pallas_call(kernel, out_shape=[jax.ShapeDtypeStruct(shape, dtype) for...  144 us
    all_to_all x3, blocking collectives, send(): return lax.all_to_all(values, 'img', 0, 0, tiled=True)  46.9 us
    all_to_all x2, blocking collectives, exchange(): return lax.all_to_all(values, BOTH, 0, 0, tiled=True)  31 us
    all_to_all x6, starting transfers between devices, exchange(): return lax.all_to_all(values, BOTH, 0, 0, tiled=True)  30.4 us
    all_to_all x6, waiting for transfers between devices, exchange(): return lax.all_to_all(values, BOTH, 0, 0, tiled=True)  28.4 us
    all_to_all x1, waiting for transfers between devices, body(): message = lax.all_to_all(message, 'img', 0, 0, tiled=True)  26 us
    all_to_all x3, waiting for transfers between devices, send(): return lax.all_to_all(values, 'img', 0, 0, tiled=True)  21.7 us
    all_to_all x3, starting transfers between devices, send(): return lax.all_to_all(values, 'img', 0, 0, tiled=True)  11 us
  transfers between devices with their start and end apart: 16, of which 11 were waited for; matrix products, arithmetic and copies ran while one was open for 7% of the time, Pallas kernels for 5%

profile of v2, /device:TPU:0, one launch (start us, length us, event | category | flops | bytes accessed | tf_op | source)
XLA Modules:
  0.0 437.6 jit_solution(3347159683224344588)
XLA Ops:
  13.4 7.4 %all-to-all-start = ((bf16[8,232,640]{2,1,0:T(8,128)(2,1)}), bf16[8,232,640]{2,1,0:T(8,128)(2,1)S(1)}, u32[]{:S(2)}, u32[]{:S(2)}) async-start(bf16[8,232,640]{2,1,0:T(8,128)(2,1)} %message.1), calls=%async_computation | async-start | bytes 4751360 | tf_op jit(solution)/shard_map/all_to_all | solution.py:792
  50.4 26.0 %all-to-all-done.refs_0_ = bf16[8,232,640]{2,1,0:T(8,128)(2,1)S(1)} async-done(((bf16[8,232,640]{2,1,0:T(8,128)(2,1)}), bf16[8,232,640]{2,1,0:T(8,128)(2,1)S(1)}, u32[]{:S(2)}, u32[]{:S(2)}) %all-to-all-start) | async-done | bytes 2375712 | tf_op jit(solution)/shard_map/all_to_all | solution.py:792
  77.8 7.6 %initial.1 = (f32[40,640]{1,0:T(8,128)}, f32[52,8,384]{2,1,0:T(8,128)}) custom-call(bf16[8,232,640]{2,1,0:T(8,128)(2,1)} %copy-done.1, bf16[24,54,320]{2,1,0:T(8,128)(2,1)} %pad_maximum_fusion.refs_1_, bf16[640,640]{1,0:T(8,128)(2,1)} %get-tuple-element.115.refs_2_.refs_5_.refs_7_.refs_13_), custom_call_target="tpu_custom_call" | custom-call | tf_op jit(solution)/shard_map/initial/pallas_call | solution.py:38
  90.5 9.4 %all-to-all-start.1 = ((f32[32,2,128]{2,1,0:T(2,128)}), f32[32,2,128]{2,1,0:T(2,128)S(1)}, u32[]{:S(2)}, u32[]{:S(2)}) async-start(f32[32,2,128]{2,1,0:T(2,128)} %bitcast.232), calls=%async_computation.1 | async-start | bytes 65536 | tf_op jit(solution)/shard_map/all_to_all | solution.py:843
  107.7 8.5 %conv2.1 = (bf16[50,64,384]{2,1,0:T(8,128)(2,1)}, f32[64,128]{1,0:T(8,128)}) custom-call(bf16[52,64,384]{2,1,0:T(8,128)(2,1)} %get-tuple-element.57.refs_0_.refs_7_.refs_1_, f32[64,128]{1,0:T(8,128)} %bitcast.184, f32[4,1,128]{2,1,0:T(1,128)} %reshape_reshape.3.refs_2_.gain_bias.refs_3_.refs_4_, bf16[3,192,192]{2,1,0:T(8,128)(2,1)} %reshape.284.refs_3_, ...), custom_call_target="tpu_custom_call" | custom-call | tf_op jit(solution)/shard_map/conv2/pallas_call | solution.py:38
  116.2 10.5 %all_to_all.126 = f32[32,2,128]{2,1,0:T(2,128)} all-to-all(f32[32,2,128]{2,1,0:T(2,128)} %bitcast.237), channel_id=1, replica_groups=mesh['img'=8,'ch'=4] {'img','ch'}, dimensions={0} | all-to-all | bytes 65536 | tf_op jit(solution)/shard_map/all_to_all | solution.py:843
  126.7 8.2 %conv3.1 = (bf16[48,64,384]{2,1,0:T(8,128)(2,1)}, f32[64,128]{1,0:T(8,128)}) custom-call(bf16[50,64,384]{2,1,0:T(8,128)(2,1)} %get-tuple-element.58.refs_0_.refs_7_.refs_1_, f32[64,128]{1,0:T(8,128)} %bitcast.199, f32[4,1,128]{2,1,0:T(1,128)} %reshape_reshape.3.refs_2_.gain_bias.refs_3_.refs_4_, bf16[3,192,192]{2,1,0:T(8,128)(2,1)} %reshape.284.refs_3_, ...), custom_call_target="tpu_custom_call" | custom-call | tf_op jit(solution)/shard_map/conv3/pallas_call | solution.py:38
  134.9 20.5 %all_to_all.127 = f32[32,2,128]{2,1,0:T(2,128)} all-to-all(f32[32,2,128]{2,1,0:T(2,128)} %bitcast.238), channel_id=1, replica_groups=mesh['img'=8,'ch'=4] {'img','ch'}, dimensions={0} | all-to-all | bytes 65536 | tf_op jit(solution)/shard_map/all_to_all | solution.py:843
  155.4 8.1 %conv4.1 = (bf16[46,64,384]{2,1,0:T(8,128)(2,1)}, f32[64,128]{1,0:T(8,128)}) custom-call(bf16[48,64,384]{2,1,0:T(8,128)(2,1)} %get-tuple-element.60.refs_0_.refs_7_.refs_1_, f32[64,128]{1,0:T(8,128)} %bitcast.203, f32[4,1,128]{2,1,0:T(1,128)} %reshape_reshape.3.refs_2_.gain_bias.refs_3_.refs_4_, bf16[3,192,192]{2,1,0:T(8,128)(2,1)} %reshape.284.refs_3_, ...), custom_call_target="tpu_custom_call" | custom-call | tf_op jit(solution)/shard_map/conv4/pallas_call | solution.py:38
  187.7 7.7 %all-to-all-done.5 = bf16[8,40,640]{2,1,0:T(8,128)(2,1)S(1)} async-done(((bf16[8,40,640]{2,1,0:T(8,128)(2,1)}), bf16[8,40,640]{2,1,0:T(8,128)(2,1)S(1)}, u32[]{:S(2)}, u32[]{:S(2)}) %all-to-all-start.5) | async-done | bytes 409632 | tf_op jit(solution)/shard_map/all_to_all | solution.py:890
  196.1 7.7 %solve1.1 = bf16[320,640]{1,0:T(8,128)(2,1)} custom-call(bf16[320,640]{1,0:T(8,128)(2,1)} %bitcast.158, bf16[640,640]{1,0:T(8,128)(2,1)} %get-tuple-element.114.refs_1_.refs_3_.refs_9_, bf16[320,640]{1,0:T(8,128)(2,1)} %bitcast.164, bf16[640,320]{1,0:T(8,128)(2,1)} %constant.153.clone.refs_6_.refs_3_.refs_5_.refs_11_, ...), custom_call_target="tpu_custom_call" | custom-call | tf_op jit(solution)/shard_map/solve1/pallas_call | solution.py:38
  203.9 16.2 %all_to_all.128 = bf16[8,40,640]{2,1,0:T(8,128)(2,1)S(1)} all-to-all(bf16[8,40,640]{2,1,0:T(8,128)(2,1)} %bitcast.180), channel_id=1, replica_groups=mesh['img'=8,'ch'=4] {'img'}, dimensions={0} | all-to-all | bytes 819200 | tf_op jit(solution)/shard_map/all_to_all | solution.py:890
  220.1 15.4 %all_to_all.129 = bf16[8,40,640]{2,1,0:T(8,128)(2,1)} all-to-all(bf16[8,40,640]{2,1,0:T(8,128)(2,1)S(1)} %broadcast_in_dim.92), channel_id=1, replica_groups=mesh['img'=8,'ch'=4] {'img'}, dimensions={0} | all-to-all | bytes 819200 | tf_op jit(solution)/shard_map/all_to_all | solution.py:890
  235.5 8.6 %solve2.1 = bf16[320,640]{1,0:T(8,128)(2,1)} custom-call(f32[1]{0:T(128)S(6)} %copy.175.refs_6_.refs_0_.penalty, bf16[320,640]{1,0:T(8,128)(2,1)} %bitcast.159, bf16[320,640]{1,0:T(8,128)(2,1)} %bitcast.174, bf16[640,640]{1,0:T(8,128)(2,1)} %get-tuple-element.114.refs_1_.refs_3_.refs_9_, bf16[320,640]{1,0:T(8,128)(2,1)} %bitcast.165, ...), custom_call_target="tpu_custom_call" | custom-call | tf_op jit(solution)/shard_map/solve2/pallas_call | solution.py:38
  244.1 15.3 %all_to_all.130 = bf16[8,40,640]{2,1,0:T(8,128)(2,1)S(1)} all-to-all(bf16[8,40,640]{2,1,0:T(8,128)(2,1)} %bitcast.179), channel_id=1, replica_groups=mesh['img'=8,'ch'=4] {'img'}, dimensions={0} | all-to-all | bytes 819200 | tf_op jit(solution)/shard_map/all_to_all | solution.py:890
  267.2 8.3 %all-to-all-done.9 = bf16[8,40,640]{2,1,0:T(8,128)(2,1)S(1)} async-done(((bf16[8,40,640]{2,1,0:T(8,128)(2,1)}), bf16[8,40,640]{2,1,0:T(8,128)(2,1)S(1)}, u32[]{:S(2)}, u32[]{:S(2)}) %all-to-all-start.9) | async-done | bytes 409632 | tf_op jit(solution)/shard_map/all_to_all | solution.py:890
  276.3 12.6 %solve3.1 = (bf16[8,48,640]{2,1,0:T(8,128)(2,1)}, f32[8,128]{1,0:T(8,128)}) custom-call(f32[1]{0:T(128)S(6)} %copy.175.refs_6_.refs_0_.penalty, f32[1]{0:T(128)} %bitcast.23.refs_1_, s32[1]{0:T(128)} %bitcast.24.refs_2_, f32[320,1]{1,0:T(8,128)} %broadcast_in_dim_reshape_squeeze.4.refs_3_, f32[1,640]{1,0:T(1,128)} %broadcast_in_dim.91.refs_4_, ...), custom_call_target="tpu_custom_call" | custom-call | tf_op jit(solution)/shard_map/solve3/pallas_call | solution.py:38
  309.3 6.4 %back5.1 = (bf16[46,64,384]{2,1,0:T(8,128)(2,1)}, f32[64,128]{1,0:T(8,128)}) custom-call(f32[46,8,384]{2,1,0:T(8,128)} %get-tuple-element.69.stacked.refs_0_, bf16[64,24]{1,0:T(8,128)(2,1)} %copy.145.weight, bf16[46,64,384]{2,1,0:T(8,128)(2,1)} %get-tuple-element.62.refs_0_.hidden_hbm.refs_1_, f32[64,128]{1,0:T(8,128)} %bitcast.196, ...), custom_call_target="tpu_custom_call" | custom-call | tf_op jit(solution)/shard_map/back5/pallas_call | solution.py:38
  326.5 10.3 %back4.1 = (bf16[46,64,384]{2,1,0:T(8,128)(2,1)}, bf16[44,64,384]{2,1,0:T(8,128)(2,1)}, f32[64,128]{1,0:T(8,128)}) custom-call(bf16[46,64,384]{2,1,0:T(8,128)(2,1)} %get-tuple-element.70.refs_0_, bf16[46,64,384]{2,1,0:T(8,128)(2,1)} %get-tuple-element.62.refs_0_.hidden_hbm.refs_1_, f32[64,128]{1,0:T(8,128)} %bitcast.198, f32[64,128]{1,0:T(8,128)} %bitcast.214, ...), custom_call_target="tpu_custom_call" | custom-call | tf_op jit(solution)/shard_map/back4/pallas_call | solution.py:38
  343.2 6.3 %wgrad4.1 = f32[192,192]{1,0:T(8,128)} custom-call(bf16[46,64,384]{2,1,0:T(8,128)(2,1)} %get-tuple-element.75.refs_0_, bf16[48,64,384]{2,1,0:T(8,128)(2,1)} %get-tuple-element.60.refs_0_.refs_7_.refs_1_, f32[64,128]{1,0:T(8,128)} %bitcast.205, f32[4,1,128]{2,1,0:T(1,128)} %reshape_reshape.3.refs_2_.gain_bias.refs_3_.refs_4_, ...), custom_call_target="tpu_custom_call" | custom-call | tf_op jit(solution)/shard_map/wgrad4/pallas_call | solution.py:38
  350.1 10.0 %back3.1 = (bf16[44,64,384]{2,1,0:T(8,128)(2,1)}, bf16[42,64,384]{2,1,0:T(8,128)(2,1)}, f32[64,128]{1,0:T(8,128)}) custom-call(bf16[44,64,384]{2,1,0:T(8,128)(2,1)} %get-tuple-element.73.refs_0_, bf16[48,64,384]{2,1,0:T(8,128)(2,1)} %get-tuple-element.60.refs_0_.refs_7_.refs_1_, f32[64,128]{1,0:T(8,128)} %bitcast.206, f32[64,128]{1,0:T(8,128)} %bitcast.216, ...), custom_call_target="tpu_custom_call" | custom-call | tf_op jit(solution)/shard_map/back3/pallas_call | solution.py:38
  368.1 6.3 %wgrad3.1 = f32[192,192]{1,0:T(8,128)} custom-call(bf16[44,64,384]{2,1,0:T(8,128)(2,1)} %get-tuple-element.79.refs_0_, bf16[50,64,384]{2,1,0:T(8,128)(2,1)} %get-tuple-element.58.refs_0_.refs_7_.refs_1_, f32[64,128]{1,0:T(8,128)} %bitcast.201, f32[4,1,128]{2,1,0:T(1,128)} %reshape_reshape.3.refs_2_.gain_bias.refs_3_.refs_4_, ...), custom_call_target="tpu_custom_call" | custom-call | tf_op jit(solution)/shard_map/wgrad3/pallas_call | solution.py:38
  375.6 10.4 %back2.1 = (f32[64,24]{1,0:T(8,128)}, bf16[42,64,384]{2,1,0:T(8,128)(2,1)}, f32[64,128]{1,0:T(8,128)}) custom-call(bf16[42,64,384]{2,1,0:T(8,128)(2,1)} %get-tuple-element.77.refs_0_, bf16[50,64,384]{2,1,0:T(8,128)(2,1)} %get-tuple-element.58.refs_0_.refs_7_.refs_1_, f32[64,128]{1,0:T(8,128)} %bitcast.202, f32[64,128]{1,0:T(8,128)} %bitcast.218, ...), custom_call_target="tpu_custom_call" | custom-call | tf_op jit(solution)/shard_map/back2/pallas_call | solution.py:38
  405.6 17.2 %all-to-all-done.14 = f32[32,43,128]{2,1,0:T(8,128)S(1)} async-done(((f32[32,43,128]{2,1,0:T(8,128)}), f32[32,43,128]{2,1,0:T(8,128)S(1)}, u32[]{:S(2)}, u32[]{:S(2)}) %all-to-all-start.14) | async-done | bytes 704544 | tf_op jit(solution)/shard_map/all_to_all | solution.py:843
  (253 shorter events, 163.9 us)
Async XLA Ops:
  13.4 63.0 %all-to-all-start = ((bf16[8,232,640]{2,1,0:T(8,128)(2,1)}), bf16[8,232,640]{2,1,0:T(8,128)(2,1)S(1)}, u32[]{:S(2)}, u32[]{:S(2)}) async-start(bf16[8,232,640]{2,1,0:T(8,128)(2,1)} %message.1), calls=%async_computation | async-start | bytes 4751360 | tf_op jit(solution)/shard_map/all_to_all | solution.py:792
  20.8 26.2 %collective-permute-start.2 = (f32[224,128]{1,0:T(8,128)S(1)}, f32[224,128]{1,0:T(8,128)}, u32[]{:S(2)}, u32[]{:S(2)}) collective-permute-start(f32[224,128]{1,0:T(8,128)S(1)} %pad_bitcast_fusion), channel_id=1, source_target_pairs={{0,1},{1,2},{2,3},{3,0},{4,5},{5,6},{6,7},{7,4},{8,9},{9,10},{10,1... | collective-permute-start | bytes 344072 | tf_op jit(solution)/shard_map/ppermute | solution.py:795
  20.8 27.1 %collective-permute-start.3 = (f32[224,128]{1,0:T(8,128)S(1)}, f32[224,128]{1,0:T(8,128)}, u32[]{:S(2)}, u32[]{:S(2)}) collective-permute-start(f32[224,128]{1,0:T(8,128)S(1)} %pad_bitcast_fusion), channel_id=1, source_target_pairs={{0,2},{1,3},{2,0},{3,1},{4,6},{5,7},{6,4},{7,5},{8,10},{9,11},{10,... | collective-permute-start | bytes 344072 | tf_op jit(solution)/shard_map/ppermute | solution.py:795
  22.4 26.5 %collective-permute-start.4 = (f32[224,128]{1,0:T(8,128)S(1)}, f32[224,128]{1,0:T(8,128)S(1)}, u32[]{:S(2)}, u32[]{:S(2)}) collective-permute-start(f32[224,128]{1,0:T(8,128)S(1)} %pad_bitcast_fusion), channel_id=1, source_target_pairs={{0,3},{1,0},{2,1},{3,2},{4,7},{5,4},{6,5},{7,6},{8,11},{9,8},{10,9... | collective-permute-start | bytes 344072 | tf_op jit(solution)/shard_map/ppermute | solution.py:795
  25.5 15.5 %collective-permute-start.1 = (bf16[24,7,320]{2,1,0:T(8,128)(2,1)}, bf16[24,7,320]{2,1,0:T(8,128)(2,1)S(1)}, u32[]{:S(2)}, u32[]{:S(2)}) collective-permute-start(bf16[24,7,320]{2,1,0:T(8,128)(2,1)} %get-tuple-element.113), channel_id=1, source_target_pairs={{4,0},{8,4},{12,8},{16,12},{20,16},{24,20},{28,24},{5,1},{9,5},{13... | collective-permute-start | bytes 322568 | tf_op jit(solution)/shard_map/ppermute | solution.py:722
  26.7 18.8 %collective-permute-start = (bf16[24,7,320]{2,1,0:T(8,128)(2,1)S(1)}, bf16[24,7,320]{2,1,0:T(8,128)(2,1)S(1)}, u32[]{:S(2)}, u32[]{:S(2)}) collective-permute-start(bf16[24,7,320]{2,1,0:T(8,128)(2,1)S(1)} %get-tuple-element.112), channel_id=1, source_target_pairs={{0,4},{4,8},{8,12},{12,16},{16,20},{20,24},{24,28},{1,5},{5,9},{9,... | collective-permute-start | bytes 322568 | tf_op jit(solution)/shard_map/ppermute | solution.py:722
  90.5 16.6 %all-to-all-start.1 = ((f32[32,2,128]{2,1,0:T(2,128)}), f32[32,2,128]{2,1,0:T(2,128)S(1)}, u32[]{:S(2)}, u32[]{:S(2)}) async-start(f32[32,2,128]{2,1,0:T(2,128)} %bitcast.232), calls=%async_computation.1 | async-start | bytes 65536 | tf_op jit(solution)/shard_map/all_to_all | solution.py:843
  163.5 10.0 %all-to-all-start.4 = ((f32[32,2,128]{2,1,0:T(2,128)}), f32[32,2,128]{2,1,0:T(2,128)S(1)}, u32[]{:S(2)}, u32[]{:S(2)}) async-start(f32[32,2,128]{2,1,0:T(2,128)} %bitcast.234), calls=%async_computation.4 | async-start | bytes 65536 | tf_op jit(solution)/shard_map/all_to_all | solution.py:843
  179.4 16.0 %all-to-all-start.5 = ((bf16[8,40,640]{2,1,0:T(8,128)(2,1)}), bf16[8,40,640]{2,1,0:T(8,128)(2,1)S(1)}, u32[]{:S(2)}, u32[]{:S(2)}) async-start(bf16[8,40,640]{2,1,0:T(8,128)(2,1)} %get-tuple-element.65), calls=%async_computation.5 | async-start | bytes 819200 | tf_op jit(solution)/shard_map/all_to_all | solution.py:890
  260.3 15.3 %all-to-all-start.9 = ((bf16[8,40,640]{2,1,0:T(8,128)(2,1)}), bf16[8,40,640]{2,1,0:T(8,128)(2,1)S(1)}, u32[]{:S(2)}, u32[]{:S(2)}) async-start(bf16[8,40,640]{2,1,0:T(8,128)(2,1)} %broadcast_in_dim.93), calls=%async_computation.9 | async-start | bytes 819200 | tf_op jit(solution)/shard_map/all_to_all | solution.py:890
  288.9 16.9 %all-to-all-start.10 = ((bf16[8,48,640]{2,1,0:T(8,128)(2,1)}), bf16[8,48,640]{2,1,0:T(8,128)(2,1)S(1)}, u32[]{:S(2)}, u32[]{:S(2)}) async-start(bf16[8,48,640]{2,1,0:T(8,128)(2,1)} %get-tuple-element.66), calls=%async_computation.10 | async-start | bytes 983040 | tf_op jit(solution)/shard_map/all_to_all | solution.py:890
  315.7 10.2 %all-to-all-start.11 = ((f32[32,2,128]{2,1,0:T(2,128)}), f32[32,2,128]{2,1,0:T(2,128)S(1)}, u32[]{:S(2)}, u32[]{:S(2)}) async-start(f32[32,2,128]{2,1,0:T(2,128)} %bitcast.236), calls=%async_computation.11 | async-start | bytes 65536 | tf_op jit(solution)/shard_map/all_to_all | solution.py:843
  336.8 12.7 %all-to-all-start.12 = ((f32[32,2,128]{2,1,0:T(2,128)}), f32[32,2,128]{2,1,0:T(2,128)S(1)}, u32[]{:S(2)}, u32[]{:S(2)}) async-start(f32[32,2,128]{2,1,0:T(2,128)} %bitcast.235), calls=%async_computation.12 | async-start | bytes 65536 | tf_op jit(solution)/shard_map/all_to_all | solution.py:843
  360.2 14.3 %all-to-all-start.13 = ((f32[32,2,128]{2,1,0:T(2,128)}), f32[32,2,128]{2,1,0:T(2,128)S(1)}, u32[]{:S(2)}, u32[]{:S(2)}) async-start(f32[32,2,128]{2,1,0:T(2,128)} %bitcast.233), calls=%async_computation.13 | async-start | bytes 65536 | tf_op jit(solution)/shard_map/all_to_all | solution.py:843
  396.2 36.1 %copy-start.28 = (f32[9,2,16]{2,1,0:T(2,128)S(1)}, f32[9,2,16]{2,1,0:T(2,128)}, u32[]{:S(2)}) copy-start(f32[9,2,16]{2,1,0:T(2,128)} %param.29) | copy-start | bytes 3460
  396.2 36.1 %copy-start.34 = (f32[9,2,16]{2,1,0:T(2,128)S(1)}, f32[9,2,16]{2,1,0:T(2,128)}, u32[]{:S(2)}) copy-start(f32[9,2,16]{2,1,0:T(2,128)} %param.37) | copy-start | bytes 3460
  396.3 36.7 %copy-start.31 = (f32[4,2,16]{2,1,0:T(2,128)S(1)}, f32[4,2,16]{2,1,0:T(2,128)}, u32[]{:S(2)}) copy-start(f32[4,2,16]{2,1,0:T(2,128)} %param.30) | copy-start | bytes 1540
  396.3 36.7 %copy-start.36 = (f32[4,2,16]{2,1,0:T(2,128)S(1)}, f32[4,2,16]{2,1,0:T(2,128)}, u32[]{:S(2)}) copy-start(f32[4,2,16]{2,1,0:T(2,128)} %param.39) | copy-start | bytes 1540
  396.3 36.7 %copy-start.37 = (f32[4,2,16]{2,1,0:T(2,128)S(1)}, f32[4,2,16]{2,1,0:T(2,128)}, u32[]{:S(2)}) copy-start(f32[4,2,16]{2,1,0:T(2,128)} %param.38) | copy-start | bytes 1540
  396.3 40.1 %copy-start.11 = (f32[3,9,16,64]{3,2,1,0:T(8,128)S(1)}, f32[3,9,16,64]{3,2,1,0:T(8,128)}, u32[]{:S(2)}) copy-start(f32[3,9,16,64]{3,2,1,0:T(8,128)} %param.28) | copy-start | bytes 331780
  396.3 40.1 %copy-start.14 = (f32[3,9,16,64]{3,2,1,0:T(8,128)S(1)}, f32[3,9,16,64]{3,2,1,0:T(8,128)}, u32[]{:S(2)}) copy-start(f32[3,9,16,64]{3,2,1,0:T(8,128)} %param.35) | copy-start | bytes 331780
  396.3 40.1 %copy-start.15 = (f32[3,9,16,64]{3,2,1,0:T(8,128)S(1)}, f32[3,9,16,64]{3,2,1,0:T(8,128)}, u32[]{:S(2)}) copy-start(f32[3,9,16,64]{3,2,1,0:T(8,128)} %param.34) | copy-start | bytes 331780
  396.3 26.5 %all-to-all-start.14 = ((f32[32,43,128]{2,1,0:T(8,128)}), f32[32,43,128]{2,1,0:T(8,128)S(1)}, u32[]{:S(2)}, u32[]{:S(2)}) async-start(f32[32,43,128]{2,1,0:T(8,128)} %pad_maximum_fusion.3), calls=%async_computation.14 | async-start | bytes 1572864 | tf_op jit(solution)/shard_map/all_to_all | solution.py:843
  425.1 11.0 %all-to-all-start.15 = ((f32[8,27,128]{2,1,0:T(8,128)}), f32[8,27,128]{2,1,0:T(8,128)S(1)}, u32[]{:S(2)}, u32[]{:S(2)}) async-start(f32[8,27,128]{2,1,0:T(8,128)} %broadcast_in_dim.101), calls=%async_computation.15 | async-start | bytes 262144 | tf_op jit(solution)/shard_map/all_to_all | solution.py:716
  (31 other events, 347.6 us)
